TPU v7x, 128 devices: a whole 4x4x4 slice. The times are simulated.
128 devices in a mesh: gx: 16 (over y, z_hi, core), gy: 8 (over x, z_lo).
Axes of the slice: x: 4, y: 4, z: 4 (z_hi: 2, z_lo: 2; z = z_hi * 2 + z_lo), core: 2. Of those that a mesh axis runs over, the one named last changes fastest.
Arguments:
- saved_mid: bfloat16 [768, 256, 256], P('gx', 'gy'), may hold values from -6 to 6
- out_grad: bfloat16 [768, 256, 256], P('gx', 'gy'), may hold values from -6 to 6
- expert_weight: bfloat16 [10, 9, 256, 256], replicated, may hold values from -0.125 to 0.125
- routes: int32 [48, 16, 4], P('gx', 'gy'), may hold values from 0 to 7, all different within a row
- gates: float32 [48, 16, 6], P('gx', 'gy'), may hold values from 0.5 to 1.5
- band_matrix: bfloat16 [16, 256, 256], replicated, may hold values from -0.375 to 0.375
- band_ids: int32 [64, 32], replicated, may hold values from 0 to 15
Outputs:
- field_grad: bfloat16 [768, 256, 256], P('gx', 'gy')
Inputs may be any that keep to these rules, and one draw needn't show every extreme that they name: `routes`: each tile names 4 different routed experts.
All inputs are finite; a program needn't handle non-finite values.
Results may differ from a plain program's by a relative error of at most 0.0095.
Values may be sent and summed in bfloat16 or wider, within the bound.
A program may use at most 128 MiB of HBM per device.

v0:
```python
import math

import jax
import jax.numpy as jnp
from jax import lax
from jax.sharding import PartitionSpec as P

SHARED = 2
TILE = 16
KH = 64
KW = 32


tap_offsets = ((-1, -1), (-1, 0), (-1, 1), (0, -1), (0, 0), (0, 1), (1, -1), (1, 0), (1, 1))


def with_halo(block, sides, width):
    for axis, dim in sides:
        count = lax.axis_size(axis)
        forward = [(i, i + 1) for i in range(count - 1)]
        backward = [(target, source) for source, target in forward]
        low = lax.ppermute(
            lax.slice_in_dim(block, block.shape[dim] - width, None, axis=dim), axis, forward
        )
        high = lax.ppermute(lax.slice_in_dim(block, 0, width, axis=dim), axis, backward)
        block = jnp.concatenate([low, block, high], axis=dim)
    return block


def passed_along(block, axis, distance):
    devices = range(lax.axis_size(axis))
    route = [(i - distance, i) for i in devices if i - distance in devices]
    return lax.ppermute(block, axis, route)


def in_blocks(value, dim, count):
    before, after = (value.shape[:dim], value.shape[dim + 1 :])
    return jnp.moveaxis(value.reshape(*before, count, -1, *after), dim, 0)


def sum_at_owner(value, axis, dim):
    parts = in_blocks(value, dim, lax.axis_size(axis))
    arrived = lax.all_to_all(parts, axis, split_axis=0, concat_axis=0, tiled=True)
    return arrived.astype(jnp.float32).sum(axis=0)


def in_order(parts, dim):
    shape = list(parts.shape[1:])
    shape[dim] *= parts.shape[0]
    return jnp.moveaxis(parts, 0, dim).reshape(shape)


def copy_for_each(value, axis):
    count = lax.axis_size(axis)
    return lax.all_to_all(
        jnp.broadcast_to(value[None], (count, *value.shape)), axis, 0, 0, tiled=True
    )


def gathered_copies(value, axis, dim):
    return in_order(copy_for_each(value, axis), dim)


def gelu_slope(values):
    normal_cdf = 0.5 * (1.0 + lax.erf(values * 0.7071067811865476))
    density = jnp.exp(-0.5 * values * values) * 0.3989422804014327
    return normal_cdf + values * density


def angle_table(index, freq, period):
    product = index[:, None] * freq[None, :] % period
    theta = product.astype(jnp.float32) * (2.0 * math.pi / period)
    return (jnp.cos(theta), jnp.sin(theta))


def body(saved_mid, out_grad, expert_weight, routes, gates, band_matrix, band_ids):
    rows_dev, cols_dev, channels = saved_mid.shape
    tiles_down = rows_dev // TILE
    tiles_across = cols_dev // TILE

    def to_tiles(field):
        depth = field.shape[-1]
        field = field.reshape(tiles_down, TILE, tiles_across, TILE, depth).transpose(0, 2, 1, 3, 4)
        return field.reshape(tiles_down * tiles_across, TILE * TILE, depth)

    extended = with_halo(saved_mid, (("gx", 0), ("gy", 1)), 1)
    patches = jnp.concatenate(
        [
            extended[1 + row_off : 1 + row_off + rows_dev, 1 + col_off : 1 + col_off + cols_dev]
            for row_off, col_off in tap_offsets
        ],
        axis=2,
    )
    patch_tiles = to_tiles(patches)
    grad_tiles = to_tiles(out_grad)
    route_rows = routes.reshape(-1, routes.shape[-1])
    gate_rows = gates.reshape(-1, gates.shape[-1])
    flat_weight = expert_weight.reshape(expert_weight.shape[0], 9 * channels, channels)

    def one_tile(pieces):
        tile_patch, tile_grad, route_row, gate_row = pieces
        chosen_ids = jnp.concatenate([jnp.arange(SHARED, dtype=jnp.int32), route_row + SHARED])
        chosen = jnp.take(flat_weight, chosen_ids, axis=0)
        preact = jnp.einsum("pk,sko->spo", tile_patch, chosen, preferred_element_type=jnp.float32)
        deltas = (
            gate_row[:, None, None] * gelu_slope(preact) * tile_grad.astype(jnp.float32)[None]
        ).astype(jnp.bfloat16)
        return jnp.einsum("spo,sko->pk", deltas, chosen, preferred_element_type=jnp.float32).astype(
            jnp.bfloat16
        )

    field = lax.map(one_tile, (patch_tiles, grad_tiles, route_rows, gate_rows))
    depth = field.shape[-1]
    field = field.reshape(tiles_down, tiles_across, TILE, TILE, depth).transpose(0, 2, 1, 3, 4)
    tap_field = field.reshape(rows_dev, cols_dev, depth)
    grad_mid = out_grad.astype(jnp.float32)
    spread = jnp.zeros((rows_dev + 2, cols_dev + 2, channels), jnp.float32)
    for tap_index, (row_off, col_off) in enumerate(tap_offsets):
        piece = tap_field[:, :, tap_index * channels : (tap_index + 1) * channels].astype(
            jnp.float32
        )
        spread = spread + jnp.pad(
            piece, ((1 + row_off, 1 - row_off), (1 + col_off, 1 - col_off), (0, 0))
        )
    from_left = passed_along(spread[:, -1].astype(jnp.bfloat16), "gy", 1).astype(jnp.float32)
    from_right = passed_along(spread[:, 0].astype(jnp.bfloat16), "gy", -1).astype(jnp.float32)
    folded = spread[:, 1:-1]
    folded = folded.at[:, 0].add(from_left).at[:, -1].add(from_right)
    from_above = passed_along(folded[-1].astype(jnp.bfloat16), "gx", 1).astype(jnp.float32)
    from_below = passed_along(folded[0].astype(jnp.bfloat16), "gx", -1).astype(jnp.float32)
    interior = folded[1:-1].at[0].add(from_above).at[-1].add(from_below)
    grad_mid = grad_mid + interior
    row_index = lax.axis_index("gx")
    col_index = lax.axis_index("gy")
    full_rows = rows_dev * lax.axis_size("gx")
    full_cols = cols_dev * lax.axis_size("gy")
    row_ids = row_index * rows_dev + jnp.arange(rows_dev, dtype=jnp.int32)
    col_ids = col_index * cols_dev + jnp.arange(cols_dev, dtype=jnp.int32)
    row_modes = jnp.arange(KH, dtype=jnp.int32)
    row_freq = jnp.where(row_modes < KH // 2, row_modes, full_rows - KH + row_modes)
    row_cos, row_sin = angle_table(row_ids, row_freq, full_rows)
    col_cos, col_sin = angle_table(col_ids, jnp.arange(KW, dtype=jnp.int32), full_cols)
    analysis_scale = 1.0 / math.sqrt(full_rows * full_cols)
    half_cos = jnp.einsum("hwc,wn->hnc", grad_mid, col_cos)
    half_sin = jnp.einsum("hwc,wn->hnc", grad_mid, col_sin)
    column_sums = sum_at_owner(jnp.stack([half_cos, half_sin]).astype(jnp.bfloat16), "gy", 2)
    coef_cos = jnp.einsum("hm,hnc->mnc", row_cos, column_sums[0]) - jnp.einsum(
        "hm,hnc->mnc", row_sin, column_sums[1]
    )
    coef_sin = jnp.einsum("hm,hnc->mnc", row_sin, column_sums[0]) + jnp.einsum(
        "hm,hnc->mnc", row_cos, column_sums[1]
    )
    owned = sum_at_owner(
        (jnp.stack([coef_cos, coef_sin]) * analysis_scale).astype(jnp.bfloat16), "gx", 1
    )
    rows_owned = owned.shape[1]
    cols_owned = owned.shape[2]
    owned_bands = lax.dynamic_slice(
        band_ids, (row_index * rows_owned, col_index * cols_owned), (rows_owned, cols_owned)
    ).reshape(-1)
    chosen = jnp.take(band_matrix, owned_bands, axis=0)
    mixed_modes = (
        jnp.einsum(
            "rjo,jio->rji",
            owned.reshape(2, rows_owned * cols_owned, channels).astype(jnp.bfloat16),
            chosen,
            preferred_element_type=jnp.float32,
        )
        .astype(jnp.bfloat16)
        .reshape(2, rows_owned, cols_owned, channels)
    )
    spectrum = gathered_copies(gathered_copies(mixed_modes, "gx", 1), "gy", 2)
    spec_cos = spectrum[0].astype(jnp.float32)
    spec_sin = spectrum[1].astype(jnp.float32)
    z_cos = jnp.einsum("mnc,hm->hnc", spec_cos, row_cos) + jnp.einsum(
        "mnc,hm->hnc", spec_sin, row_sin
    )
    z_sin = jnp.einsum("mnc,hm->hnc", spec_sin, row_cos) - jnp.einsum(
        "mnc,hm->hnc", spec_cos, row_sin
    )
    spectral = jnp.einsum("hnc,wn->hwc", z_cos, col_cos) + jnp.einsum("hnc,wn->hwc", z_sin, col_sin)
    spectral = spectral / math.sqrt(2 * KH * KW)
    return (grad_mid + spectral).astype(jnp.bfloat16)


def solution(mesh):
    placed = (
        P("gx", "gy", None),
        P("gx", "gy", None),
        P(),
        P("gx", "gy", None),
        P("gx", "gy", None),
        P(),
        P(),
    )
    return jax.shard_map(
        body, mesh=mesh, in_specs=placed, out_specs=P("gx", "gy", None), check_vma=False
    )
```

profile of v0, /device:TPU:0, one launch (start us, length us, event | category | flops | bytes accessed | tf_op | source)
XLA Modules:
  0.0 326.8 jit_solution(6496662318228767424)
XLA Ops:
  4.7 4.8 %collective-permute-done.1 = bf16[1,32,256]{2,1,0:T(8,128)(2,1)S(1)} collective-permute-done((bf16[1,32,256]{2,1,0:T(8,128)(2,1)S(1)}, bf16[1,32,256]{2,1,0:T(8,128)(2,1)S(1)}, u32[]{:S(2)}, u32[]{:S(2)}) %collective-permute-start.1) | collective-permute-done | bytes 16416 | tf_op jit(solution)/shard_map/ppermute | solution.py:25
  9.6 2.9 collective-permute-start.2
  16.4 4.3 %collective-permute-done.3 = bf16[50,1,256]{2,1,0:T(2,128)(2,1)S(1)} collective-permute-done((bf16[50,1,256]{2,1,0:T(2,128)(2,1)S(1)}, bf16[50,1,256]{2,1,0:T(2,128)(2,1)S(1)}, u32[]{:S(2)}, u32[]{:S(2)}) %collective-permute-start.3) | collective-permute-done | bytes 25632 | tf_op jit(solution)/shard_map/ppermute | solution.py:25
  22.9 3.5 %copy.104 = bf16[3,16,2,16,2304]{4,3,1,2,0:T(8,128)(2,1)} copy(bf16[3,16,2,16,2304]{4,3,2,1,0:T(8,128)(2,1)S(1)} %bitcast.169) | data formatting | bytes 14155776 | tf_op jit(solution)/shard_map/reshape | solution.py:83
  26.5 147.2 %while.14 = (s32[]{:T(128)}, bf16[6,256,2304]{2,1,0:T(8,128)(2,1)}, f32[6,6]{1,0:T(8,128)S(1)}, s32[6,4]{1,0:T(8,128)S(1)}, bf16[10,2304,256]{2,1,0:T(8,128)(2,1...) while((s32[]{:T(128)}, bf16[6,256,2304]{2,1,0:T(8,128)(2,1)}, ...), condition=%wide.region_1.2_spmd, body=%wide.region_0.1_spmd.sunk | while | flops 3635938304 | bytes 31857488 | solution.py:112
  26.6 8.8 %gather_fusion = bf16[6,2304,256]{2,1,0:T(8,128)(2,1)} fusion(bf16[10,2304,256]{2,1,0:T(8,128)(2,1)} %get-tuple-element.230, s32[1024]{0:T(1024)S(1)} %pad_clamp_fusion.3), kind=kCustom, calls=%fused_computation.clone.1 | custom fusion | bytes 14155800 | tf_op jit(solution)/shard_map/while/body/eval_jaxpr/jit(_take)/gather | solution.py:103
  36.5 14.6 %fusion.210 = bf16[6,256,2304]{2,1,0:T(8,128)(2,1)} fusion(bf16[6,256,2304]{2,1,0:T(8,128)(2,1)} %get-tuple-element.219, s32[]{:T(128)} %get-tuple-element.218, bf16[6,2304,256]{2,1,0:T(8,128)(2,1)} %gather_fusion, pred[6]{0:T(512)(128)(4,1)S(1)} %compare_and_fusion.3, bf16[6,256,2304]{2,1,0:T(8,128)(2,1)} %get-tuple-element.231, ...), kind=kOutput, calls=%fused_computation.6.clone.1 | convolution fusion | flops 3635871744 | bytes 16779776 | tf_op jit(solution)/shard_map/while/body/eval_jaxpr/spo,sko->pk/dot_general | solution.py:108
  51.1 8.7 %gather_fusion = bf16[6,2304,256]{2,1,0:T(8,128)(2,1)} fusion(bf16[10,2304,256]{2,1,0:T(8,128)(2,1)} %get-tuple-element.230, s32[1024]{0:T(1024)S(1)} %pad_clamp_fusion.3), kind=kCustom, calls=%fused_computation.clone.1 | custom fusion | bytes 14155800 | tf_op jit(solution)/shard_map/while/body/eval_jaxpr/jit(_take)/gather | solution.py:103
  61.0 14.6 %fusion.210 = bf16[6,256,2304]{2,1,0:T(8,128)(2,1)} fusion(bf16[6,256,2304]{2,1,0:T(8,128)(2,1)} %get-tuple-element.219, s32[]{:T(128)} %get-tuple-element.218, bf16[6,2304,256]{2,1,0:T(8,128)(2,1)} %gather_fusion, pred[6]{0:T(512)(128)(4,1)S(1)} %compare_and_fusion.3, bf16[6,256,2304]{2,1,0:T(8,128)(2,1)} %get-tuple-element.231, ...), kind=kOutput, calls=%fused_computation.6.clone.1 | convolution fusion | flops 3635871744 | bytes 16779776 | tf_op jit(solution)/shard_map/while/body/eval_jaxpr/spo,sko->pk/dot_general | solution.py:108
  75.7 8.8 %gather_fusion = bf16[6,2304,256]{2,1,0:T(8,128)(2,1)} fusion(bf16[10,2304,256]{2,1,0:T(8,128)(2,1)} %get-tuple-element.230, s32[1024]{0:T(1024)S(1)} %pad_clamp_fusion.3), kind=kCustom, calls=%fused_computation.clone.1 | custom fusion | bytes 14155800 | tf_op jit(solution)/shard_map/while/body/eval_jaxpr/jit(_take)/gather | solution.py:103
  85.6 14.5 %fusion.210 = bf16[6,256,2304]{2,1,0:T(8,128)(2,1)} fusion(bf16[6,256,2304]{2,1,0:T(8,128)(2,1)} %get-tuple-element.219, s32[]{:T(128)} %get-tuple-element.218, bf16[6,2304,256]{2,1,0:T(8,128)(2,1)} %gather_fusion, pred[6]{0:T(512)(128)(4,1)S(1)} %compare_and_fusion.3, bf16[6,256,2304]{2,1,0:T(8,128)(2,1)} %get-tuple-element.231, ...), kind=kOutput, calls=%fused_computation.6.clone.1 | convolution fusion | flops 3635871744 | bytes 16779776 | tf_op jit(solution)/shard_map/while/body/eval_jaxpr/spo,sko->pk/dot_general | solution.py:108
  100.2 8.8 %gather_fusion = bf16[6,2304,256]{2,1,0:T(8,128)(2,1)} fusion(bf16[10,2304,256]{2,1,0:T(8,128)(2,1)} %get-tuple-element.230, s32[1024]{0:T(1024)S(1)} %pad_clamp_fusion.3), kind=kCustom, calls=%fused_computation.clone.1 | custom fusion | bytes 14155800 | tf_op jit(solution)/shard_map/while/body/eval_jaxpr/jit(_take)/gather | solution.py:103
  110.1 14.5 %fusion.210 = bf16[6,256,2304]{2,1,0:T(8,128)(2,1)} fusion(bf16[6,256,2304]{2,1,0:T(8,128)(2,1)} %get-tuple-element.219, s32[]{:T(128)} %get-tuple-element.218, bf16[6,2304,256]{2,1,0:T(8,128)(2,1)} %gather_fusion, pred[6]{0:T(512)(128)(4,1)S(1)} %compare_and_fusion.3, bf16[6,256,2304]{2,1,0:T(8,128)(2,1)} %get-tuple-element.231, ...), kind=kOutput, calls=%fused_computation.6.clone.1 | convolution fusion | flops 3635871744 | bytes 16779776 | tf_op jit(solution)/shard_map/while/body/eval_jaxpr/spo,sko->pk/dot_general | solution.py:108
  124.8 8.8 %gather_fusion = bf16[6,2304,256]{2,1,0:T(8,128)(2,1)} fusion(bf16[10,2304,256]{2,1,0:T(8,128)(2,1)} %get-tuple-element.230, s32[1024]{0:T(1024)S(1)} %pad_clamp_fusion.3), kind=kCustom, calls=%fused_computation.clone.1 | custom fusion | bytes 14155800 | tf_op jit(solution)/shard_map/while/body/eval_jaxpr/jit(_take)/gather | solution.py:103
  134.7 14.5 %fusion.210 = bf16[6,256,2304]{2,1,0:T(8,128)(2,1)} fusion(bf16[6,256,2304]{2,1,0:T(8,128)(2,1)} %get-tuple-element.219, s32[]{:T(128)} %get-tuple-element.218, bf16[6,2304,256]{2,1,0:T(8,128)(2,1)} %gather_fusion, pred[6]{0:T(512)(128)(4,1)S(1)} %compare_and_fusion.3, bf16[6,256,2304]{2,1,0:T(8,128)(2,1)} %get-tuple-element.231, ...), kind=kOutput, calls=%fused_computation.6.clone.1 | convolution fusion | flops 3635871744 | bytes 16779776 | tf_op jit(solution)/shard_map/while/body/eval_jaxpr/spo,sko->pk/dot_general | solution.py:108
  149.3 8.8 %gather_fusion = bf16[6,2304,256]{2,1,0:T(8,128)(2,1)} fusion(bf16[10,2304,256]{2,1,0:T(8,128)(2,1)} %get-tuple-element.230, s32[1024]{0:T(1024)S(1)} %pad_clamp_fusion.3), kind=kCustom, calls=%fused_computation.clone.1 | custom fusion | bytes 14155800 | tf_op jit(solution)/shard_map/while/body/eval_jaxpr/jit(_take)/gather | solution.py:103
  159.2 14.5 %fusion.210 = bf16[6,256,2304]{2,1,0:T(8,128)(2,1)} fusion(bf16[6,256,2304]{2,1,0:T(8,128)(2,1)} %get-tuple-element.219, s32[]{:T(128)} %get-tuple-element.218, bf16[6,2304,256]{2,1,0:T(8,128)(2,1)} %gather_fusion, pred[6]{0:T(512)(128)(4,1)S(1)} %compare_and_fusion.3, bf16[6,256,2304]{2,1,0:T(8,128)(2,1)} %get-tuple-element.231, ...), kind=kOutput, calls=%fused_computation.6.clone.1 | convolution fusion | flops 3635871744 | bytes 16779776 | tf_op jit(solution)/shard_map/while/body/eval_jaxpr/spo,sko->pk/dot_general | solution.py:108
  173.7 5.2 %copy.107 = bf16[3,2,16,16,2304]{4,2,0,3,1:T(8,128)(2,1)S(1)} copy(bf16[3,2,16,16,2304]{4,3,2,1,0:T(8,128)(2,1)} %bitcast.172) | data formatting | bytes 14155776 | tf_op jit(solution)/shard_map/reshape | solution.py:114
  179.6 3.4 %fusion.191 = (bf16[50,34,256]{2,0,1:T(8,128)(2,1)S(1)}, f32[50,34,256]{2,0,1:T(8,128)}) fusion(bf16[48,32,256]{2,0,1:T(8,128)(2,1)S(1)} %get-tuple-element.145, bf16[48,32,256]{2,0,1:T(8,128)(2,1)S(1)} %get-tuple-element.146, bf16[48,32,256]{2,0,1:T(8,128)(2,1)S(1)} %get-tuple-element.147, bf16[48,32,256]{2,0,1:T(8,128)(2,1)S(1)} %get-tuple-element.148, ...), kind=kLoop, calls=%fused_computation.228 | loop fusion | flops 7833600 | bytes 9689088 | tf_op jit(solution)/shard_map/convert.33
  183.0 4.8 %collective-permute-start.4 = (bf16[50,256]{1,0:T(8,128)(2,1)S(1)}, bf16[50,256]{1,0:T(8,128)(2,1)S(1)}, u32[]{:S(2)}, u32[]{:S(2)}) collective-permute-start(bf16[50,256]{1,0:T(8,128)(2,1)S(1)} %get-tuple-element.156), channel_id=1, source_target_pairs={{0,1},{1,2},{2,3},{3,4},{4,5},{5,6},{6,7},{8,9},{9,10},{10,11},{11... | collective-permute-start | bytes 76808 | tf_op jit(solution)/shard_map/ppermute | solution.py:33
  195.3 2.3 scatter-add.15
  199.3 3.0 collective-permute-start.6
  204.0 4.1 %collective-permute-done.7 = bf16[32,256]{1,0:T(8,128)(2,1)S(1)} collective-permute-done((bf16[32,256]{1,0:T(8,128)(2,1)S(1)}, bf16[32,256]{1,0:T(8,128)(2,1)S(1)}, u32[]{:S(2)}, u32[]{:S(2)}) %collective-permute-start.7) | collective-permute-done | bytes 16416 | tf_op jit(solution)/shard_map/ppermute | solution.py:33
  211.0 2.4 stack.18
  213.4 2.4 stack.19
  215.8 3.4 %copy_bitcast_fusion.1 = bf16[8,2,48,4,256]{4,3,2,1,0:T(4,128)(2,1)} fusion(bf16[1,48,8,4,256]{4,3,2,1,0:T(4,128)(2,1)} %stack.19, bf16[1,48,8,4,256]{4,3,2,1,0:T(4,128)(2,1)} %stack.18), kind=kLoop, calls=%fused_computation.58 | loop fusion | flops 786432 | bytes 3145728 | tf_op jit(solution)/shard_map/transpose | solution.py:38
  219.2 4.7 %all-to-all-start = ((bf16[8,2,48,4,256]{4,3,2,1,0:T(4,128)(2,1)}), bf16[8,2,48,4,256]{4,3,2,1,0:T(4,128)(2,1)}, u32[]{:S(2)}, u32[]{:S(2)}) async-start(bf16[8,2,48,4,256]{4,3,2,1,0:T(4,128)(2,1)} %copy_bitcast_fusion.1), calls=%async_computation | async-start | bytes 3145728 | tf_op jit(solution)/shard_map/all_to_all | solution.py:43
  224.8 21.0 %all-to-all-done = bf16[8,2,48,4,256]{4,3,2,1,0:T(4,128)(2,1)} async-done(((bf16[8,2,48,4,256]{4,3,2,1,0:T(4,128)(2,1)}), bf16[8,2,48,4,256]{4,3,2,1,0:T(4,128)(2,1)}, u32[]{:S(2)}, u32[]{:S(2)}) %all-to-all-start) | async-done | bytes 1572896 | tf_op jit(solution)/shard_map/all_to_all | solution.py:43
  256.5 10.5 %all-to-all-start.1 = ((bf16[16,2,4,4,256]{4,2,3,1,0:T(4,128)(2,1)}), bf16[16,2,4,4,256]{4,2,3,1,0:T(4,128)(2,1)S(1)}, u32[]{:S(2)}, u32[]{:S(2)}) async-start(bf16[16,2,4,4,256]{4,2,3,1,0:T(4,128)(2,1)} %fusion.70), calls=%async_computation.1 | async-start | bytes 524288 | tf_op jit(solution)/shard_map/all_to_all | solution.py:43
  269.1 7.1 %all-to-all-done.1 = bf16[16,2,4,4,256]{4,2,3,1,0:T(4,128)(2,1)S(1)} async-done(((bf16[16,2,4,4,256]{4,2,3,1,0:T(4,128)(2,1)}), bf16[16,2,4,4,256]{4,2,3,1,0:T(4,128)(2,1)S(1)}, u32[]{:S(2)}, u32[]{:S(2)}) %all-to-all-start.1) | async-done | bytes 262176 | tf_op jit(solution)/shard_map/all_to_all | solution.py:43
  278.7 12.0 %all_to_all.20 = bf16[16,2,4,4,256]{4,3,2,1,0:T(4,128)(2,1)S(1)} all-to-all(bf16[16,2,4,4,256]{4,3,2,1,0:T(4,128)(2,1)S(1)} %broadcast_in_dim.51), channel_id=1, replica_groups=mesh['gx'=16,'gy'=8] {'gx'}, dimensions={0} | all-to-all | bytes 524288 | tf_op jit(solution)/shard_map/all_to_all | solution.py:55
  291.1 29.9 %all_to_all.21 = bf16[8,2,64,4,256]{4,2,3,1,0:T(8,128)(2,1)S(1)} all-to-all(bf16[8,2,64,4,256]{4,2,3,1,0:T(8,128)(2,1)S(1)} %broadcast_in_dim.53), channel_id=1, replica_groups=mesh['gx'=16,'gy'=8] {'gy'}, dimensions={0} | all-to-all | bytes 4194304 | tf_op jit(solution)/shard_map/all_to_all | solution.py:55
  (154 shorter events, 54.7 us)
Async XLA Ops:
  0.0 267.1 %copy-start = (bf16[16,256,256]{2,1,0:T(8,128)(2,1)S(1)}, bf16[16,256,256]{2,1,0:T(8,128)(2,1)}, u32[]{:S(2)}) copy-start(bf16[16,256,256]{2,1,0:T(8,128)(2,1)} %param.22) | copy-start | bytes 6291460
  0.9 2.6 collective-permute-start
  2.2 7.3 %collective-permute-start.1 = (bf16[1,32,256]{2,1,0:T(8,128)(2,1)S(1)}, bf16[1,32,256]{2,1,0:T(8,128)(2,1)S(1)}, u32[]{:S(2)}, u32[]{:S(2)}) collective-permute-start(bf16[1,32,256]{2,1,0:T(8,128)(2,1)S(1)} %get-tuple-element.161), channel_id=1, source_target_pairs={{8,0},{16,8},{24,16},{32,24},{40,32},{48,40},{56,48},{64,56},{72,6... | collective-permute-start | bytes 49160 | tf_op jit(solution)/shard_map/ppermute | solution.py:25
  3.5 11.1 %copy-start.6 = (f32[3,2,6]{2,1,0:T(2,128)S(1)}, f32[3,2,6]{2,1,0:T(2,128)}, u32[]{:S(2)}) copy-start(f32[3,2,6]{2,1,0:T(2,128)} %param.21) | copy-start | bytes 436
  3.5 11.1 %copy-start.7 = (s32[3,2,4]{2,1,0:T(2,128)S(1)}, s32[3,2,4]{2,1,0:T(2,128)}, u32[]{:S(2)}) copy-start(s32[3,2,4]{2,1,0:T(2,128)} %param.20) | copy-start | bytes 292
  9.6 6.5 %collective-permute-start.2 = (bf16[50,1,256]{2,1,0:T(2,128)(2,1)S(1)}, bf16[50,1,256]{2,1,0:T(2,128)(2,1)S(1)}, u32[]{:S(2)}, u32[]{:S(2)}) collective-permute-start(bf16[50,1,256]{2,1,0:T(2,128)(2,1)S(1)} %get-tuple-element.160), channel_id=1, source_target_pairs={{0,1},{1,2},{2,3},{3,4},{4,5},{5,6},{6,7},{8,9},{9,10},{10,11},{11... | collective-permute-start | bytes 76808 | tf_op jit(solution)/shard_map/ppermute | solution.py:22
  14.6 1.7 copy-start.4
  14.6 6.1 %collective-permute-start.3 = (bf16[50,1,256]{2,1,0:T(2,128)(2,1)S(1)}, bf16[50,1,256]{2,1,0:T(2,128)(2,1)S(1)}, u32[]{:S(2)}, u32[]{:S(2)}) collective-permute-start(bf16[50,1,256]{2,1,0:T(2,128)(2,1)S(1)} %get-tuple-element.159), channel_id=1, source_target_pairs={{1,0},{2,1},{3,2},{4,3},{5,4},{6,5},{7,6},{9,8},{10,9},{11,10},{12... | collective-permute-start | bytes 76808 | tf_op jit(solution)/shard_map/ppermute | solution.py:25
  183.0 7.7 %collective-permute-start.4 = (bf16[50,256]{1,0:T(8,128)(2,1)S(1)}, bf16[50,256]{1,0:T(8,128)(2,1)S(1)}, u32[]{:S(2)}, u32[]{:S(2)}) collective-permute-start(bf16[50,256]{1,0:T(8,128)(2,1)S(1)} %get-tuple-element.156), channel_id=1, source_target_pairs={{0,1},{1,2},{2,3},{3,4},{4,5},{5,6},{6,7},{8,9},{9,10},{10,11},{11... | collective-permute-start | bytes 76808 | tf_op jit(solution)/shard_map/ppermute | solution.py:33
  189.5 5.8 %collective-permute-start.5 = (bf16[50,256]{1,0:T(8,128)(2,1)S(1)}, bf16[50,256]{1,0:T(8,128)(2,1)S(1)}, u32[]{:S(2)}, u32[]{:S(2)}) collective-permute-start(bf16[50,256]{1,0:T(8,128)(2,1)S(1)} %get-tuple-element.155), channel_id=1, source_target_pairs={{1,0},{2,1},{3,2},{4,3},{5,4},{6,5},{7,6},{9,8},{10,9},{11,10},{12... | collective-permute-start | bytes 76808 | tf_op jit(solution)/shard_map/ppermute | solution.py:33
  197.7 4.7 %copy-start.3 = (f32[50,32,256]{2,1,0:T(8,128)S(1)}, f32[50,32,256]{2,1,0:T(8,128)}, u32[]{:S(2)}) copy-start(f32[50,32,256]{2,1,0:T(8,128)} %scatter-add.15) | copy-start | bytes 4915204
  199.3 4.6 %collective-permute-start.6 = (bf16[32,256]{1,0:T(8,128)(2,1)S(1)}, bf16[32,256]{1,0:T(8,128)(2,1)S(1)}, u32[]{:S(2)}, u32[]{:S(2)}) collective-permute-start(bf16[32,256]{1,0:T(8,128)(2,1)S(1)} %get-tuple-element.158), channel_id=1, source_target_pairs={{0,8},{8,16},{16,24},{24,32},{32,40},{40,48},{48,56},{56,64},{64,7... | collective-permute-start | bytes 49160 | tf_op jit(solution)/shard_map/ppermute | solution.py:33
  202.4 5.7 %copy-start.5 = (bf16[48,32,256]{2,1,0:T(8,128)(2,1)S(1)}, bf16[48,32,256]{2,1,0:T(8,128)(2,1)}, u32[]{:S(2)}) copy-start(bf16[48,32,256]{2,1,0:T(8,128)(2,1)} %param.18) | copy-start | bytes 2359300
  202.5 5.6 %collective-permute-start.7 = (bf16[32,256]{1,0:T(8,128)(2,1)S(1)}, bf16[32,256]{1,0:T(8,128)(2,1)S(1)}, u32[]{:S(2)}, u32[]{:S(2)}) collective-permute-start(bf16[32,256]{1,0:T(8,128)(2,1)S(1)} %get-tuple-element.157), channel_id=1, source_target_pairs={{8,0},{16,8},{24,16},{32,24},{40,32},{48,40},{56,48},{64,56},{72,6... | collective-permute-start | bytes 49160 | tf_op jit(solution)/shard_map/ppermute | solution.py:33
  208.1 1.4 copy-start.1
  219.2 26.6 %all-to-all-start = ((bf16[8,2,48,4,256]{4,3,2,1,0:T(4,128)(2,1)}), bf16[8,2,48,4,256]{4,3,2,1,0:T(4,128)(2,1)}, u32[]{:S(2)}, u32[]{:S(2)}) async-start(bf16[8,2,48,4,256]{4,3,2,1,0:T(4,128)(2,1)} %copy_bitcast_fusion.1), calls=%async_computation | async-start | bytes 3145728 | tf_op jit(solution)/shard_map/all_to_all | solution.py:43
  256.5 19.7 %all-to-all-start.1 = ((bf16[16,2,4,4,256]{4,2,3,1,0:T(4,128)(2,1)}), bf16[16,2,4,4,256]{4,2,3,1,0:T(4,128)(2,1)S(1)}, u32[]{:S(2)}, u32[]{:S(2)}) async-start(bf16[16,2,4,4,256]{4,2,3,1,0:T(4,128)(2,1)} %fusion.70), calls=%async_computation.1 | async-start | bytes 524288 | tf_op jit(solution)/shard_map/all_to_all | solution.py:43
  323.7 1.4 copy-start.2
where the time goes:
time: 328 us; the launch traced here: 327 us
  matrix products  101 us (31%)
  local copies, waits for them, and re-layouts  90.6 us (28%)
  waiting for transfers between devices  43.2 us (13%)
  blocking collectives  41.9 us (13%)
  starting transfers between devices  32.7 us (10%)
  other arithmetic  16.5 us (5%)
    dot_general x6, matrix products, one_tile(): jnp.einsum('spo,sko->pk', deltas, chosen, preferred_element_type=jnp.floa...  87.3 us
    gather x6, local copies, waits for them, and re-layouts, one_tile(): chosen = jnp.take(flat_weight, chosen_ids, axis=0)  52.4 us
    all_to_all x2, blocking collectives, copy_for_each(): lax.all_to_all(jnp.broadcast_to(value[None], (count, *value.shape)), axis...  41.9 us
    all_to_all x2, waiting for transfers between devices, sum_at_owner(): lax.all_to_all(parts, axis, split_axis=0, concat_axis=0, tiled=True)  28 us
    all_to_all x2, starting transfers between devices, sum_at_owner(): lax.all_to_all(parts, axis, split_axis=0, concat_axis=0, tiled=True)  15.2 us
    ppermute x4, starting transfers between devices, passed_along(): return lax.ppermute(block, axis, route)  10.6 us
    ppermute x2, waiting for transfers between devices, with_halo(): lax.ppermute(lax.slice_in_dim(block, 0, width, axis=dim), axis, backward)  9.1 us
  transfers between devices with their start and end apart: 10, of which 6 were waited for; matrix products, arithmetic and copies ran while one was open for 3% of the time, Pallas kernels for 0%

commit v1 on v0

v1 whole, which is shorter than its diff:
```python
import math

import jax
import jax.numpy as jnp
import numpy as np
from jax import lax
from jax.experimental import pallas as pl
from jax.experimental.pallas import tpu as pltpu
from jax.sharding import PartitionSpec as P

F32 = jnp.float32
BF = jnp.bfloat16
MESH = pl.DeviceIdType.MESH
GX, GY = 16, 8
ROWS, COLS, CH = 48, 32, 256
KH, KW = 64, 32
H, W = 768, 256
EXPERTS, SLOTS, TILES = 10, 6, 6

DIRS = ((1, 0), (-1, 0), (0, 1), (0, -1), (1, 1), (1, -1), (-1, 1), (-1, -1))


def mod(value, count):
    return lax.rem(value + count, count)


def tables():
    n = 4 * np.arange(8)[None, :] + np.arange(4)[:, None]
    theta = 2 * np.pi * ((n.reshape(-1)[:, None] * np.arange(W)[None, :]) % W) / W
    col = np.concatenate([np.cos(theta), np.sin(theta)])
    m = np.arange(KH)
    freq = np.where(m < KH // 2, m, H - KH + m)
    phase = 2 * np.pi * ((freq[:, None] * np.arange(H)[None, :]) % H) / H
    rc = np.cos(phase).reshape(2, 32, GX, ROWS)
    rs = np.sin(phase).reshape(2, 32, GX, ROWS)
    top = np.stack([rc, -rs], axis=3)
    bottom = np.stack([rs, rc], axis=3)
    row = np.stack([top, bottom], axis=1)
    row = row.transpose(3, 0, 1, 2, 4, 5).reshape(GX, 128, 2 * ROWS)
    return col, row


COL_TABLE, ROW_TABLE = tables()


def gelu_slope(values):
    normal_cdf = 0.5 * (1.0 + lax.erf(values * 0.7071067811865476))
    density = jnp.exp(-0.5 * values * values) * 0.3989422804014327
    return normal_cdf + values * density


def transpose_blocks(parts):
    lane = lax.broadcasted_iota(jnp.int32, parts[0].shape, parts[0].ndim - 1)
    axis = parts[0].ndim - 1
    low = lane < 64
    a, b, c, d = parts
    a, c = (
        jnp.where(low, a, pltpu.roll(c, 64, axis)),
        jnp.where(low, pltpu.roll(a, 64, axis), c),
    )
    b, d = (
        jnp.where(low, b, pltpu.roll(d, 64, axis)),
        jnp.where(low, pltpu.roll(b, 64, axis), d),
    )
    even = (lane & 32) == 0
    a, b = (
        jnp.where(even, a, pltpu.roll(b, 32, axis)),
        jnp.where(even, pltpu.roll(a, 96, axis), b),
    )
    c, d = (
        jnp.where(even, c, pltpu.roll(d, 32, axis)),
        jnp.where(even, pltpu.roll(c, 96, axis), d),
    )
    return a, b, c, d


def border_copies(gx, gy, sources, targets, send_sem, recv_sem):
    copies = []
    for k, (dr, dc) in enumerate(DIRS):
        copies.append(
            pltpu.make_async_remote_copy(
                src_ref=sources[k],
                dst_ref=targets[k],
                send_sem=send_sem.at[k],
                recv_sem=recv_sem.at[k],
                device_id=(mod(gx + dr, GX), mod(gy + dc, GY)),
                device_id_type=MESH,
            )
        )
    return copies


def greet(devices):
    barrier = pltpu.get_barrier_semaphore()
    for device in devices:
        pl.semaphore_signal(barrier, inc=1, device_id=device, device_id_type=MESH)
    pl.semaphore_wait(barrier, len(devices))


def neighbours(gx, gy):
    return [(mod(gx + dr, GX), mod(gy + dc, GY)) for dr, dc in DIRS]


def halo_body(mid, shifted, ext, ecol, ecor, rrow, rcol, rcor, side, ssem, rsem):
    gx, gy = lax.axis_index("gx"), lax.axis_index("gy")
    ext[1 : ROWS + 1] = mid[...].astype(F32)
    ecol[0] = ext[1 : ROWS + 1, COLS - 1, :].astype(BF)
    ecol[1] = ext[1 : ROWS + 1, 0, :].astype(BF)
    for k, (r, c) in enumerate(((ROWS, COLS - 1), (ROWS, 0), (1, COLS - 1), (1, 0))):
        ecor[k] = jnp.broadcast_to(ext[r, c : c + 1, :], (16, CH)).astype(BF)
    greet(neighbours(gx, gy))
    sources = [mid.at[ROWS - 1], mid.at[0], ecol.at[0], ecol.at[1]]
    sources += [ecor.at[k] for k in range(4)]
    targets = [rrow.at[0], rrow.at[1], rcol.at[0], rcol.at[1]]
    targets += [rcor.at[k] for k in range(4)]
    copies = border_copies(gx, gy, sources, targets, ssem, rsem)
    for copy in copies:
        copy.start()
    for copy in copies:
        copy.wait()
    above = jnp.where(gx > 0, 1.0, 0.0)
    below = jnp.where(gx < GX - 1, 1.0, 0.0)
    left = jnp.where(gy > 0, 1.0, 0.0)
    right = jnp.where(gy < GY - 1, 1.0, 0.0)
    ext[0] = rrow[0].astype(F32) * above
    ext[ROWS + 1] = rrow[1].astype(F32) * below
    side[0, 8 : 8 + ROWS] = rcol[0].astype(F32) * left
    side[1, 8 : 8 + ROWS] = rcol[1].astype(F32) * right
    side[0, 7:8] = rcor[0][0:1].astype(F32) * (above * left)
    side[1, 7:8] = rcor[1][0:1].astype(F32) * (above * right)
    side[0, 8 + ROWS : 9 + ROWS] = rcor[2][0:1].astype(F32) * (below * left)
    side[1, 8 + ROWS : 9 + ROWS] = rcor[3][0:1].astype(F32) * (below * right)
    place = lax.broadcasted_iota(jnp.int32, (COLS, CH), 0)

    def one_row(r, _):
        row = ext[r]
        before = side[0, pl.ds(r + 7, 1), :]
        after = side[1, pl.ds(r + 7, 1), :]
        shifted[1, r] = row.astype(BF)
        shifted[0, r] = jnp.where(place == 0, before, pltpu.roll(row, 1, 0)).astype(BF)
        shifted[2, r] = jnp.where(place == COLS - 1, after, pltpu.roll(row, COLS - 1, 0)).astype(BF)
        return 0

    lax.fori_loop(0, ROWS + 2, one_row, 0, unroll=5)


def tile_body(routes, gates, shifted, grad, w_hbm, spread, w, deltas, pre_a, pre_b, wsem):
    copies = [pltpu.make_async_copy(w_hbm.at[e], w.at[e], wsem.at[e]) for e in range(EXPERTS)]
    for copy in copies:
        copy.start()

    def expert(t, s):
        route = routes[t // 2, t % 2, jnp.maximum(s - 2, 0)]
        return jnp.where(s < 2, s, route + 2)

    def window(t):
        return t // 2, pl.ds(pl.multiple_of((t % 2) * 16, 16), 16)

    def forward(i, out):
        s, t = i // TILES, i % TILES
        rt, cols = window(t)
        pieces = [
            shifted[b, pl.ds(rt * 16 + a, 16), cols, :].reshape(256, CH)
            for a in range(3)
            for b in range(3)
        ]
        out[...] = jnp.dot(
            jnp.concatenate(pieces, axis=1), w[expert(t, s)], preferred_element_type=F32
        )

    def slope(i, src):
        s, t = i // TILES, i % TILES
        rt, cols = window(t)
        g = grad[pl.ds(rt * 16, 16), cols, :].reshape(256, CH).astype(F32)
        deltas[t, s] = (gates[rt, t % 2, s] * gelu_slope(src[...]) * g).astype(BF)

    copies[0].wait()
    copies[1].wait()
    forward(0, pre_a)

    def step(k, _):
        i = 2 * k
        forward(i + 1, pre_b)
        slope(i, pre_a)
        forward(i + 2, pre_a)
        slope(i + 1, pre_b)
        return 0

    lax.fori_loop(0, 5, step, 0)
    forward(11, pre_b)
    slope(10, pre_a)
    for copy in copies[2:]:
        copy.wait()
    forward(12, pre_a)
    slope(11, pre_b)
    lax.fori_loop(6, 17, step, 0)
    forward(35, pre_b)
    slope(34, pre_a)
    slope(35, pre_b)
    spread[...] = jnp.zeros_like(spread)

    def backward(t, _):
        rt, cols = window(t)
        d = jnp.concatenate([deltas[t, s] for s in range(SLOTS)], axis=1)
        chosen = [expert(t, s) for s in range(SLOTS)]
        for a in range(3):
            for b in range(3):
                tap = 3 * a + b
                kernels = jnp.concatenate(
                    [w[e, tap * CH : (tap + 1) * CH, :] for e in chosen], axis=1
                )
                r = lax.dot_general(
                    d, kernels, (((1,), (1,)), ((), ())), preferred_element_type=F32
                )
                spread[b, pl.ds(rt * 16 + a, 16), cols, :] += r.reshape(16, 16, CH)
        return 0

    lax.fori_loop(0, TILES, backward, 0)


def spectral_body(
    spread, grad, col, col_t, row, row_t, band_hbm, band_ids, out,
    total, erow, ecol, ecor, rrow, rcol, rcor,
    xs, xr, half, cs, cr, cg, sp, zs, fs, fr, band,
    border_s, border_r, x_s, x_r, c_s, c_r, g_s, g_r, p_s, p_r, f_s, f_r, band_sem,
):
    gx, gy = lax.axis_index("gx"), lax.axis_index("gy")
    band_copy = pltpu.make_async_copy(
        band_hbm.at[:, pl.ds(pl.multiple_of(gy * 32, 32), 32), :], band, band_sem
    )
    band_copy.start()
    place = lax.broadcasted_iota(jnp.int32, (COLS, CH), 0)

    def joined(r):
        ahead = jnp.where(place > 0, pltpu.roll(spread[2, r], 1, 0), 0.0)
        behind = jnp.where(place < COLS - 1, pltpu.roll(spread[0, r], COLS - 1, 0), 0.0)
        return spread[1, r] + ahead + behind

    erow[0] = joined(ROWS + 1).astype(BF)
    erow[1] = joined(0).astype(BF)
    ecol[0] = spread[2, 1 : ROWS + 1, COLS - 1, :].astype(BF)
    ecol[1] = spread[0, 1 : ROWS + 1, 0, :].astype(BF)
    for k, (b, r, c) in enumerate(
        ((2, ROWS + 1, COLS - 1), (0, ROWS + 1, 0), (2, 0, COLS - 1), (0, 0, 0))
    ):
        ecor[k] = jnp.broadcast_to(spread[b, r, c : c + 1, :], (16, CH)).astype(BF)
    others_y = [(gx, mod(gy + d, GY)) for d in range(1, GY)]
    others_x = [(mod(gx + d, GX), gy) for d in range(1, GX)]
    greet(others_y + others_x + neighbours(gx, gy)[4:])
    sources = [erow.at[0], erow.at[1], ecol.at[0], ecol.at[1]]
    sources += [ecor.at[k] for k in range(4)]
    targets = [rrow.at[0], rrow.at[1], rcol.at[0], rcol.at[1]]
    targets += [rcor.at[k] for k in range(4)]
    copies = border_copies(gx, gy, sources, targets, border_s, border_r)
    for copy in copies:
        copy.start()

    def own_row(r, _):
        total[r] = joined(r + 1) + grad[r].astype(F32)
        return 0

    lax.fori_loop(0, ROWS, own_row, 0, unroll=4)
    for copy in copies:
        copy.wait()
    above = jnp.where(gx > 0, 1.0, 0.0)
    below = jnp.where(gx < GX - 1, 1.0, 0.0)
    left = jnp.where(gy > 0, 1.0, 0.0)
    right = jnp.where(gy < GY - 1, 1.0, 0.0)
    total[0] += rrow[0].astype(F32) * above
    total[ROWS - 1] += rrow[1].astype(F32) * below
    total[:, 0, :] += rcol[0].astype(F32) * left
    total[:, COLS - 1, :] += rcol[1].astype(F32) * right
    total[0, 0:1, :] += rcor[0][0:1].astype(F32) * (above * left)
    total[0, COLS - 1 : COLS, :] += rcor[1][0:1].astype(F32) * (above * right)
    total[ROWS - 1, 0:1, :] += rcor[2][0:1].astype(F32) * (below * left)
    total[ROWS - 1, COLS - 1 : COLS, :] += rcor[3][0:1].astype(F32) * (below * right)

    def along_y(source, target, d, send, recv):
        return pltpu.make_async_remote_copy(
            src_ref=source,
            dst_ref=target,
            send_sem=send.at[d],
            recv_sem=recv.at[d],
            device_id=(gx, mod(gy + d, GY)),
            device_id_type=MESH,
        )

    def along_x(source, target, d, send, recv):
        return pltpu.make_async_remote_copy(
            src_ref=source,
            dst_ref=target,
            send_sem=send.at[d],
            recv_sem=recv.at[d],
            device_id=(mod(gx + d, GX), gy),
            device_id_type=MESH,
        )

    def split_rows(g, _):
        for jt in range(2):
            lanes = slice(jt * 128, jt * 128 + 128)
            parts = [total[4 * g + q, :, lanes] for q in range(4)]
            for s, part in enumerate(transpose_blocks(parts)):
                xs[jt * 4 + s, g] = part.astype(BF)
        return 0

    lax.fori_loop(0, 12, split_rows, 0, unroll=2)
    for d in range(1, GY):
        along_y(xs.at[mod(gy + d, GY)], xr.at[gy], d, x_s, x_r).start()
    xr[gy] = xs[gy]
    for d in range(1, GY):
        along_y(xs.at[mod(gy + d, GY)], xr.at[mod(gy - d, GY)], d, x_s, x_r).wait()

    for pair in range(6):
        data = jnp.concatenate(
            [xr[:, 2 * pair + k].reshape(256, 128) for k in range(2)], axis=1
        )
        c = jnp.dot(col[...], data, preferred_element_type=F32)
        for k in range(2):
            g = 2 * pair + k
            for part in range(2):
                parts = [
                    c[part * 32 + 8 * p : part * 32 + 8 * p + 8, k * 128 : k * 128 + 128]
                    for p in range(4)
                ]
                for q, block in enumerate(transpose_blocks(parts)):
                    half[pl.ds(part * ROWS + 4 * g + q, 8, stride=2 * ROWS), :] = block
    forward_scale = 1.0 / math.sqrt(H * W)
    for pair in range(4):
        data = jnp.concatenate(
            [half[(2 * pair + k) * 96 : (2 * pair + k + 1) * 96].astype(BF) for k in range(2)],
            axis=1,
        )
        c = jnp.dot(row[gx], data, preferred_element_type=F32) * forward_scale
        for k in range(2):
            for mh in range(2):
                cs[mh * 8 + 2 * pair + k] = c[
                    mh * 64 : mh * 64 + 64, k * 128 : k * 128 + 128
                ].astype(BF)
    for d in range(1, GX):
        along_x(cs.at[mod(gx + d, GX)], cr.at[gx], d, c_s, c_r).start()
    cr[gx] = cs[gx]
    for d in range(1, GX):
        along_x(cs.at[mod(gx + d, GX)], cr.at[mod(gx - d, GX)], d, c_s, c_r).wait()
    coef = cr[0].astype(F32)
    for k in range(1, GX):
        coef = coef + cr[k].astype(F32)
    cg[gy] = coef.astype(BF)
    for d in range(1, GY):
        along_y(cg.at[gy], cg.at[gy], d, g_s, g_r).start()
    band_copy.wait()
    for d in range(1, GY):
        along_y(cg.at[gy], cg.at[mod(gy - d, GY)], d, g_s, g_r).wait()

    inputs = []
    for jt in range(2):
        parts = [cg[jt * 4 + p].astype(F32) for p in range(4)]
        inputs.append(transpose_blocks(parts))
    n8 = lax.rem(gx, 8)
    mh = gx // 8
    ids = band_ids[pl.ds(pl.multiple_of(mh * 32, 32), 32), :]
    column = lax.broadcasted_iota(jnp.int32, (32, KW), 1)
    block_of_lane = lax.broadcasted_iota(jnp.int32, (64, 512), 1) >> 5
    lane_block = lax.broadcasted_iota(jnp.int32, (64, 128), 1) >> 5
    mixer = band[...].reshape(512, CH)
    spec = jnp.zeros((64, 128), F32)
    for n4 in range(4):
        modes = jnp.concatenate([inputs[0][n4], inputs[1][n4]], axis=1).astype(BF)
        z = lax.dot_general(
            modes, mixer, (((1,), (1,)), ((), ())), preferred_element_type=F32
        )
        mine = jnp.sum(jnp.where(column == 4 * n8 + n4, ids, 0), axis=1, keepdims=True)
        mine = jnp.concatenate([mine, mine], axis=0)
        z = jnp.where(block_of_lane == mine, z, 0.0)
        y = z[:, 0:128] + z[:, 128:256] + z[:, 256:384] + z[:, 384:512]
        y = y + pltpu.roll(y, 64, 1)
        y = y + pltpu.roll(y, 32, 1)
        spec = jnp.where(lane_block == n4, y, spec)
    sp[gx] = spec.astype(BF)
    for d in range(1, GX):
        along_x(sp.at[gx], sp.at[gx], d, p_s, p_r).start()
    for d in range(1, GX):
        along_x(sp.at[gx], sp.at[mod(gx - d, GX)], d, p_s, p_r).wait()

    inverse_scale = 1.0 / math.sqrt(2 * KH * KW)
    for pair in range(4):
        data = jnp.concatenate(
            [
                jnp.concatenate([sp[2 * pair + k], sp[8 + 2 * pair + k]], axis=0)
                for k in range(2)
            ],
            axis=1,
        )
        z = jnp.dot(row_t[gx], data, preferred_element_type=F32) * inverse_scale
        for k in range(2):
            zs[(2 * pair + k) * 96 : (2 * pair + k + 1) * 96, :] = z[:, k * 128 : k * 128 + 128]
    for pair in range(6):
        columns = []
        for k in range(2):
            g = 2 * pair + k
            pieces = []
            for part in range(2):
                parts = [
                    zs[pl.ds(part * ROWS + 4 * g + q, 8, stride=2 * ROWS), :] for q in range(4)
                ]
                pieces += list(transpose_blocks(parts))
            columns.append(jnp.concatenate(pieces, axis=0))
        data = jnp.concatenate(columns, axis=1).astype(BF)
        f = jnp.dot(col_t[...], data, preferred_element_type=F32)
        for k in range(2):
            for j in range(8):
                fs[j, 2 * pair + k] = f[j * 32 : j * 32 + 32, k * 128 : k * 128 + 128].astype(BF)
    for d in range(1, GY):
        along_y(fs.at[mod(gy + d, GY)], fr.at[gy], d, f_s, f_r).start()
    fr[gy] = fs[gy]
    for d in range(1, GY):
        along_y(fs.at[mod(gy + d, GY)], fr.at[mod(gy - d, GY)], d, f_s, f_r).wait()

    def join_rows(g, _):
        for jt in range(2):
            lanes = slice(jt * 128, jt * 128 + 128)
            parts = [fr[jt * 4 + s, g].astype(F32) for s in range(4)]
            for q, part in enumerate(transpose_blocks(parts)):
                out[4 * g + q, :, lanes] = (total[4 * g + q, :, lanes] + part).astype(BF)
        return 0

    lax.fori_loop(0, 12, join_rows, 0, unroll=2)


VMEM = pl.BlockSpec(memory_space=pltpu.VMEM)
SMEM = pl.BlockSpec(memory_space=pltpu.SMEM)
ANY = pl.BlockSpec(memory_space=pl.ANY)


def dma(count):
    return pltpu.SemaphoreType.DMA((count,))


BORDER_SCRATCH = [
    pltpu.VMEM((2, COLS, CH), BF),
    pltpu.VMEM((2, ROWS, CH), BF),
    pltpu.VMEM((4, 16, CH), BF),
]


def body(saved_mid, out_grad, expert_weight, routes, gates, band_matrix, band_ids):
    shifted = pl.pallas_call(
        halo_body,
        name="halo",
        out_shape=jax.ShapeDtypeStruct((3, ROWS + 2, COLS, CH), BF),
        in_specs=[VMEM],
        out_specs=VMEM,
        scratch_shapes=[
            pltpu.VMEM((ROWS + 2, COLS, CH), F32),
            pltpu.VMEM((2, ROWS, CH), BF),
            pltpu.VMEM((4, 16, CH), BF),
            *BORDER_SCRATCH,
            pltpu.VMEM((2, 64, CH), F32),
            dma(8),
            dma(8),
        ],
        compiler_params=pltpu.CompilerParams(collective_id=0, has_side_effects=True),
    )(saved_mid)
    spread = pl.pallas_call(
        tile_body,
        name="tiles",
        out_shape=jax.ShapeDtypeStruct((3, ROWS + 2, COLS, CH), F32),
        in_specs=[SMEM, SMEM, VMEM, VMEM, ANY],
        out_specs=VMEM,
        scratch_shapes=[
            pltpu.VMEM((EXPERTS, 9 * CH, CH), BF),
            pltpu.VMEM((TILES, SLOTS, 256, CH), BF),
            pltpu.VMEM((256, CH), F32),
            pltpu.VMEM((256, CH), F32),
            dma(EXPERTS),
        ],
        compiler_params=pltpu.CompilerParams(vmem_limit_bytes=56 * 2**20),
    )(routes, gates, shifted, out_grad, expert_weight.reshape(EXPERTS, 9 * CH, CH))
    col = jnp.asarray(COL_TABLE, BF)
    row = jnp.asarray(ROW_TABLE, BF)
    return pl.pallas_call(
        spectral_body,
        name="spectral",
        out_shape=jax.ShapeDtypeStruct((ROWS, COLS, CH), BF),
        in_specs=[VMEM] * 6 + [ANY, VMEM],
        out_specs=VMEM,
        scratch_shapes=[
            pltpu.VMEM((ROWS, COLS, CH), F32),
            pltpu.VMEM((2, COLS, CH), BF),
            pltpu.VMEM((2, ROWS, CH), BF),
            pltpu.VMEM((4, 16, CH), BF),
            *BORDER_SCRATCH,
            pltpu.VMEM((GY, 12, 32, 128), BF),
            pltpu.VMEM((GY, 12, 32, 128), BF),
            pltpu.VMEM((8 * 96, 128), F32),
            pltpu.VMEM((GX, 64, 128), BF),
            pltpu.VMEM((GX, 64, 128), BF),
            pltpu.VMEM((GY, 64, 128), BF),
            pltpu.VMEM((GX, 64, 128), BF),
            pltpu.VMEM((8 * 96, 128), F32),
            pltpu.VMEM((GY, 12, 32, 128), BF),
            pltpu.VMEM((GY, 12, 32, 128), BF),
            pltpu.VMEM((16, 32, CH), BF),
            dma(8), dma(8), dma(GY), dma(GY), dma(GX), dma(GX), dma(GY), dma(GY),
            dma(GX), dma(GX), dma(GY), dma(GY), pltpu.SemaphoreType.DMA,
        ],
        compiler_params=pltpu.CompilerParams(
            collective_id=1, has_side_effects=True, vmem_limit_bytes=56 * 2**20
        ),
    )(
        spread, out_grad, col, jnp.asarray(COL_TABLE.T, BF), row,
        jnp.asarray(ROW_TABLE.transpose(0, 2, 1), BF), band_matrix, band_ids,
    )


def solution(mesh):
    placed = (
        P("gx", "gy", None),
        P("gx", "gy", None),
        P(),
        P("gx", "gy", None),
        P("gx", "gy", None),
        P(),
        P(),
    )
    return jax.shard_map(
        body, mesh=mesh, in_specs=placed, out_specs=P("gx", "gy", None), check_vma=False
    )
```

time: 328 us -> 113 us (0.34)
  Pallas kernels: 0 us -> 109 us
  matrix products: 101 us -> 0 us
  local copies, waits for them, and re-layouts: 90.6 us -> 2.77 us
  waiting for transfers between devices: 43.2 us -> 0 us
  blocking collectives: 41.9 us -> 0 us
  starting transfers between devices: 32.7 us -> 0 us
  other arithmetic: 16.5 us -> 0 us
    pallas_call x0 -> x3, Pallas kernels: none -> 109 us  [the longest x1 57.7 us: body(): pl.pallas_call(spectral_body, name='spectral', out_shape=jax.ShapeDtypeSt...]
    dot_general x19 -> x0, matrix products: 101 us -> none  [the longest x6 87.3 us: one_tile(): jnp.einsum('spo,sko->pk', deltas, chosen, preferred_element_type=jnp.floa...]
    gather x7 -> x0, local copies, waits for them, and re-layouts: 54.4 us -> none  [the longest x6 52.4 us: one_tile(): chosen = jnp.take(flat_weight, chosen_ids, axis=0)]
    all_to_all x2 -> x0, blocking collectives: 41.9 us -> none  [copy_for_each(): lax.all_to_all(jnp.broadcast_to(value[None], (count, *value.shape)), axis...]
    all_to_all x2 -> x0, waiting for transfers between devices: 28 us -> none  [sum_at_owner(): lax.all_to_all(parts, axis, split_axis=0, concat_axis=0, tiled=True)]
    ppermute x8 -> x0, starting transfers between devices: 17.5 us -> none  [the longest x4 10.6 us: passed_along(): return lax.ppermute(block, axis, route)]
    all_to_all x2 -> x0, starting transfers between devices: 15.2 us -> none  [sum_at_owner(): lax.all_to_all(parts, axis, split_axis=0, concat_axis=0, tiled=True)]
    ppermute x8 -> x0, waiting for transfers between devices: 15.2 us -> none  [the longest x2 9.1 us: with_halo(): lax.ppermute(lax.slice_in_dim(block, 0, width, axis=dim), axis, backward)]
  transfers between devices with their start and end apart: 10 -> 0, of which waited for: 6 -> 0; matrix products, arithmetic and copies ran while one was open for 3% -> 0% of each run, Pallas kernels for 0% -> 0%
where the time goes in v1:
time: 113 us; the launch traced here: 112 us
  Pallas kernels  109 us (96%)
  local copies, waits for them, and re-layouts  2.77 us (2%)
    pallas_call x1, Pallas kernels, body(): pl.pallas_call(spectral_body, name='spectral', out_shape=jax.ShapeDtypeSt...  57.7 us
    pallas_call x1, Pallas kernels, body(): pl.pallas_call(tile_body, name='tiles', out_shape=jax.ShapeDtypeStruct((3...  36.2 us
    pallas_call x1, Pallas kernels, body(): pl.pallas_call(halo_body, name='halo', out_shape=jax.ShapeDtypeStruct((3,...  14.8 us
    unnamed x4, local copies, waits for them, and re-layouts  2.77 us

profile of v1, /device:TPU:0, one launch (start us, length us, event | category | flops | bytes accessed | tf_op | source)
XLA Modules:
  0.0 111.5 jit_solution(2474333760149936868)
XLA Ops:
  0.0 14.8 %halo.1.shifted = bf16[3,50,32,256]{3,2,1,0:T(8,128)(2,1)} custom-call(bf16[48,32,256]{2,1,0:T(8,128)(2,1)} %mid.1), custom_call_target="tpu_custom_call" | custom-call | tf_op jit(solution)/shard_map/halo/pallas_call | solution.py:446
  14.8 0.0 copy-start
  14.8 36.2 %tiles.1.spread = f32[3,50,32,256]{3,2,1,0:T(8,128)} custom-call(s32[3,2,4]{2,1,0:T(2,128)} %routes.1, f32[3,2,6]{2,1,0:T(2,128)} %gates.1, bf16[3,50,32,256]{3,2,1,0:T(8,128)(2,1)} %halo.1.shifted, bf16[48,32,256]{2,1,0:T(8,128)(2,1)} %grad.3, bf16[10,2304,256]{2,1,0:T(8,128)(2,1)} %bitcast.1), custom_call_target="tpu_custom_call" | custom-call | tf_op jit(solution)/shard_map/tiles/pallas_call | solution.py:463
  51.1 0.0 copy-done
  51.1 0.7 copy.12.band_ids
  51.8 57.7 %spectral.1 = bf16[48,32,256]{2,1,0:T(8,128)(2,1)} custom-call(f32[3,50,32,256]{3,2,1,0:T(8,128)} %tiles.1.spread, bf16[48,32,256]{2,1,0:T(8,128)(2,1)} %grad.3, bf16[64,256]{1,0:T(8,128)(2,1)} %constant.8.clone.col, bf16[256,64]{1,0:T(8,128)(2,1)} %constant.10.clone.col_t, bf16[16,128,96]{2,1,0:T(8,128)(2,1)} %constant.9.clone.row, ...), custom_call_target="tpu_custom_call" | custom-call | tf_op jit(solution)/shard_map/spectral/pallas_call | solution.py:480
  109.4 2.1 %copy.14 = bf16[48,32,256]{2,1,0:T(8,128)(2,1)} copy(bf16[48,32,256]{2,1,0:T(8,128)(2,1)} %spectral.1) | data formatting | bytes 1572864
Async XLA Ops:
  14.8 36.3 %copy-start = (s32[64,32]{0,1:T(8,128)S(1)}, s32[64,32]{0,1:T(8,128)}, u32[]{:S(2)}) copy-start(s32[64,32]{0,1:T(8,128)} %param.17) | copy-start | bytes 24580

commit v2 on v1

v2 whole, which is shorter than its diff:
```python
import math

import jax
import jax.numpy as jnp
import numpy as np
from jax import lax
from jax.experimental import pallas as pl
from jax.experimental.pallas import tpu as pltpu
from jax.sharding import PartitionSpec as P

F32 = jnp.float32
BF = jnp.bfloat16
MESH = pl.DeviceIdType.MESH
GX, GY = 16, 8
ROWS, COLS, CH = 48, 32, 256
KH, KW = 64, 32
H, W = 768, 256
EXPERTS, SLOTS, TILES = 10, 6, 6
OPEN = ROWS + 4
CHUNKS = ((0, 4, 0), (4, 4, 144), (8, 5, 288))

DIRS = ((1, 0), (-1, 0), (0, 1), (0, -1), (1, 1), (1, -1), (-1, 1), (-1, -1))


def mod(value, count):
    return lax.rem(value + count, count)


def tables():
    n = (4 * np.arange(8)[None, :] + np.arange(4)[:, None]).reshape(-1)

    def wave(columns):
        theta = 2 * np.pi * ((n[:, None] * columns[None, :]) % W) / W
        return np.concatenate([np.cos(theta), np.sin(theta)])

    col = wave(np.arange(W))
    edge = np.zeros((5, 64, GY, 16))
    for j in range(GY):
        for side, column in enumerate((COLS * j - 1, COLS * j + COLS)):
            if 0 <= column < W:
                for g in range(5):
                    edge[g, :, j, side * 8 + g] = wave(np.array([column]))[:, 0]
    m = np.arange(KH)
    freq = np.where(m < KH // 2, m, H - KH + m)
    row = np.zeros((GX, 2, 2, 32, 2, OPEN))
    for gx in range(GX):
        h = ROWS * gx - 1 + np.arange(OPEN)
        phase = 2 * np.pi * ((freq[:, None] * h[None, :]) % H) / H
        keep = (h >= 0) & (h < H) & (np.arange(OPEN) < ROWS + 2)
        rc = (np.cos(phase) * keep).reshape(2, 32, OPEN)
        rs = (np.sin(phase) * keep).reshape(2, 32, OPEN)
        row[gx, :, 0, :, 0], row[gx, :, 0, :, 1] = rc, -rs
        row[gx, :, 1, :, 0], row[gx, :, 1, :, 1] = rs, rc
    back = row[..., 1 : ROWS + 1].reshape(GX, 128, 2 * ROWS).transpose(0, 2, 1)
    return col, edge.reshape(320, 128), row.reshape(GX, 128, 2 * OPEN), back


COL_TABLE, EDGE_TABLE, ROW_TABLE, BACK_TABLE = tables()


def gelu_slope_twice(values):
    density = jnp.exp2((values * values) * (-0.5 * math.log2(math.e)))
    return (1.0 + lax.erf(values * math.sqrt(0.5))) + (values * math.sqrt(2.0 / math.pi)) * density


def transpose_blocks(parts):
    lane = lax.broadcasted_iota(jnp.int32, parts[0].shape, parts[0].ndim - 1)
    axis = parts[0].ndim - 1
    low = lane < 64
    a, b, c, d = parts
    a, c = (
        jnp.where(low, a, pltpu.roll(c, 64, axis)),
        jnp.where(low, pltpu.roll(a, 64, axis), c),
    )
    b, d = (
        jnp.where(low, b, pltpu.roll(d, 64, axis)),
        jnp.where(low, pltpu.roll(b, 64, axis), d),
    )
    even = (lane & 32) == 0
    a, b = (
        jnp.where(even, a, pltpu.roll(b, 32, axis)),
        jnp.where(even, pltpu.roll(a, 96, axis), b),
    )
    c, d = (
        jnp.where(even, c, pltpu.roll(d, 32, axis)),
        jnp.where(even, pltpu.roll(c, 96, axis), d),
    )
    return a, b, c, d


def border_copies(gx, gy, sources, targets, send_sem, recv_sem):
    copies = []
    for k, (dr, dc) in enumerate(DIRS):
        copies.append(
            pltpu.make_async_remote_copy(
                src_ref=sources[k],
                dst_ref=targets[k],
                send_sem=send_sem.at[k],
                recv_sem=recv_sem.at[k],
                device_id=(mod(gx + dr, GX), mod(gy + dc, GY)),
                device_id_type=MESH,
            )
        )
    return copies


def fused_body(
    mid, grad_hbm, w_hbm, routes, gates, band_hbm, band_ids, col, col_t, edge_table, row_hbm, back_hbm,
    out,
    grad, w, row, back, band, ext, shifted, side, deltas, spread, total, edge, edges,
    erow, ecol, ecor, rrow, rcol, rcor, brow, bcol, bcor, hrow, hcol, hcor,
    xs, xr, half, cs, cr, cg, sp, zs, fs, fr,
    w_sem, in_sem, halo_s, halo_r, border_s, border_r,
    x_s, x_r, c_s, c_r, g_s, g_r, p_s, p_r, f_s, f_r,
):
    gx, gy = lax.axis_index("gx"), lax.axis_index("gy")
    w_copies = [pltpu.make_async_copy(w_hbm.at[e], w.at[e], w_sem.at[e]) for e in range(EXPERTS)]
    in_copies = [
        pltpu.make_async_copy(grad_hbm, grad, in_sem.at[0]),
        pltpu.make_async_copy(row_hbm.at[gx], row, in_sem.at[1]),
        pltpu.make_async_copy(back_hbm.at[gx], back, in_sem.at[2]),
        pltpu.make_async_copy(
            band_hbm.at[:, pl.ds(pl.multiple_of(gy * 32, 32), 32), :], band, in_sem.at[3]
        ),
    ]
    w_copies[0].start()
    in_copies[0].start()
    for copy in w_copies[1:] + in_copies[1:]:
        copy.start()
    barrier = pltpu.get_barrier_semaphore()
    partners = [(gx, mod(gy + d, GY)) for d in range(1, GY)]
    partners += [(mod(gx + d, GX), gy) for d in range(1, GX)]
    partners += [(mod(gx + dr, GX), mod(gy + dc, GY)) for dr, dc in DIRS[4:]]
    for device in partners:
        pl.semaphore_signal(barrier, inc=1, device_id=device, device_id_type=MESH)

    above = jnp.where(gx > 0, 1.0, 0.0)
    below = jnp.where(gx < GX - 1, 1.0, 0.0)
    left = jnp.where(gy > 0, 1.0, 0.0)
    right = jnp.where(gy < GY - 1, 1.0, 0.0)

    ext[1 : ROWS + 1] = mid[...].astype(F32)
    hcol[0] = ext[1 : ROWS + 1, COLS - 1, :].astype(BF)
    hcol[1] = ext[1 : ROWS + 1, 0, :].astype(BF)
    for k, (r, c) in enumerate(((ROWS, COLS - 1), (ROWS, 0), (1, COLS - 1), (1, 0))):
        hcor[k] = jnp.broadcast_to(ext[r, c : c + 1, :], (16, CH)).astype(BF)
    pl.semaphore_wait(barrier, len(partners))
    halo = border_copies(
        gx, gy,
        [mid.at[ROWS - 1], mid.at[0], hcol.at[0], hcol.at[1]] + [hcor.at[k] for k in range(4)],
        [rrow.at[0], rrow.at[1], rcol.at[0], rcol.at[1]] + [rcor.at[k] for k in range(4)],
        halo_s, halo_r,
    )
    for copy in halo:
        copy.start()
    spread[...] = jnp.zeros_like(spread)
    edges[...] = jnp.zeros_like(edges)
    for copy in halo:
        copy.wait()
    ext[0] = rrow[0].astype(F32) * above
    ext[ROWS + 1] = rrow[1].astype(F32) * below
    side[0, 8 : 8 + ROWS] = rcol[0].astype(F32) * left
    side[1, 8 : 8 + ROWS] = rcol[1].astype(F32) * right
    side[0, 7:8] = rcor[0][0:1].astype(F32) * (above * left)
    side[1, 7:8] = rcor[1][0:1].astype(F32) * (above * right)
    side[0, 8 + ROWS : 9 + ROWS] = rcor[2][0:1].astype(F32) * (below * left)
    side[1, 8 + ROWS : 9 + ROWS] = rcor[3][0:1].astype(F32) * (below * right)
    place = lax.broadcasted_iota(jnp.int32, (COLS, CH), 0)

    def shift_row(r, _):
        line = ext[r]
        before = side[0, pl.ds(r + 7, 1), :]
        after = side[1, pl.ds(r + 7, 1), :]
        shifted[1, r] = line.astype(BF)
        shifted[0, r] = jnp.where(place == 0, before, pltpu.roll(line, 1, 0)).astype(BF)
        shifted[2, r] = jnp.where(place == COLS - 1, after, pltpu.roll(line, COLS - 1, 0)).astype(BF)
        return 0

    lax.fori_loop(0, ROWS + 2, shift_row, 0, unroll=5)

    def expert(t, s):
        return routes[t // 2, t % 2, s - 2] + 2

    def forward(s, kernel_of):
        for t in range(TILES):
            rt, cols = t // 2, slice((t % 2) * 16, (t % 2) * 16 + 16)
            pieces = [
                shifted[b, rt * 16 + a : rt * 16 + a + 16, cols, :].reshape(256, CH)
                for a in range(3)
                for b in range(3)
            ]
            pre = jnp.dot(
                jnp.concatenate(pieces, axis=1), w[kernel_of(t, s)], preferred_element_type=F32
            )
            g = grad[rt * 16 : rt * 16 + 16, cols, :].reshape(256, CH).astype(F32)
            gate = gates[rt, t % 2, s] * 0.5
            deltas[t, s] = (gelu_slope_twice(pre) * (g * gate)).astype(BF)

    def forward_shared(s, _):
        forward(s, lambda t, s: s)
        return 0

    def forward_routed(s, _):
        forward(s, expert)
        return 0

    in_copies[0].wait()
    w_copies[0].wait()
    w_copies[1].wait()
    lax.fori_loop(0, 2, forward_shared, 0)
    for copy in w_copies[2:]:
        copy.wait()
    lax.fori_loop(2, SLOTS, forward_routed, 0)

    def along_y(source, target, d, send, recv):
        return pltpu.make_async_remote_copy(
            src_ref=source, dst_ref=target, send_sem=send, recv_sem=recv,
            device_id=(gx, mod(gy + d, GY)), device_id_type=MESH,
        )

    def along_x(source, target, d, send, recv):
        return pltpu.make_async_remote_copy(
            src_ref=source, dst_ref=target, send_sem=send, recv_sem=recv,
            device_id=(mod(gx + d, GX), gy), device_id_type=MESH,
        )

    def backward(t, _):
        rt, cols = t // 2, pl.ds(pl.multiple_of((t % 2) * 16, 16), 16)
        d = jnp.concatenate([deltas[t, s] for s in range(SLOTS)], axis=1)
        chosen = [0, 1] + [expert(t, s) for s in range(2, SLOTS)]
        for a in range(3):
            for b in range(3):
                tap = 3 * a + b
                kernels = jnp.concatenate(
                    [w[e, tap * CH : (tap + 1) * CH, :] for e in chosen], axis=1
                )
                r = lax.dot_general(
                    d, kernels, (((1,), (1,)), ((), ())), preferred_element_type=F32
                )
                spread[b, pl.ds(rt * 16 + a, 16), cols, :] += r.reshape(16, 16, CH)
        return 0

    def joined(r):
        ahead = jnp.where(place > 0, pltpu.roll(spread[2, r], 1, 0), 0.0)
        behind = jnp.where(place < COLS - 1, pltpu.roll(spread[0, r], COLS - 1, 0), 0.0)
        return spread[1, r] + ahead + behind

    def x_copies(chunk, target):
        _, groups, start = CHUNKS[chunk]
        rows = slice(start, start + groups * 32 + 16)
        return [
            along_y(
                xs.at[mod(gy + d, GY), rows], xr.at[target(d), rows], d,
                x_s.at[chunk, d], x_r.at[chunk, d],
            )
            for d in range(1, GY)
        ]

    for chunk, (first, groups, start) in enumerate(CHUNKS):
        lax.fori_loop(2 * chunk, 2 * chunk + 2, backward, 0)

        def split_group(k, _):
            g = first + k
            for q in range(4):
                r = 4 * g + q
                keep = jnp.where((r >= 1) & (r <= ROWS), 1.0, 0.0)
                field = grad[jnp.clip(r - 1, 0, ROWS - 1)].astype(F32)
                total[r] = joined(r) + field * keep
            for jt in range(2):
                lanes = slice(jt * 128, jt * 128 + 128)
                parts = [total[4 * g + q, :, lanes] for q in range(4)]
                for s, part in enumerate(transpose_blocks(parts)):
                    rows = pl.ds(pl.multiple_of(start + 32 * k, 16), 32)
                    xs[jt * 4 + s, rows, :] = part.astype(BF)
            return 0

        lax.fori_loop(0, groups, split_group, 0)
        rows = slice(4 * first, 4 * first + 4 * groups)
        for jt in range(2):
            lanes = slice(jt * 128, jt * 128 + 128)
            edge[0, jt, rows] = spread[0, rows, 0, lanes]
            edge[1, jt, rows] = spread[2, rows, COLS - 1, lanes]
            for q in range(4):
                for s in range(2):
                    edges[q, jt, s * 8 : s * 8 + groups] = edge[
                        s, jt, pl.ds(4 * first + q, groups, stride=4), :
                    ]
            for s, part in enumerate(transpose_blocks([edges[q, jt] for q in range(4)])):
                last = start + groups * 32
                xs[jt * 4 + s, last : last + 16, :] = part.astype(BF)
        for copy in x_copies(chunk, lambda d: gy):
            copy.start()

    erow[0] = total[ROWS + 1].astype(BF)
    erow[1] = total[0].astype(BF)
    for jt in range(2):
        lanes = slice(jt * 128, jt * 128 + 128)
        ecol[0, :, lanes] = edge[1, jt, 1 : ROWS + 1].astype(BF)
        ecol[1, :, lanes] = edge[0, jt, 1 : ROWS + 1].astype(BF)
        for k, (s, r) in enumerate(((1, ROWS + 1), (0, ROWS + 1), (1, 0), (0, 0))):
            ecor[k, :, lanes] = jnp.broadcast_to(edge[s, jt, r : r + 1, :], (16, 128)).astype(BF)
    border = border_copies(
        gx, gy,
        [erow.at[0], erow.at[1], ecol.at[0], ecol.at[1]] + [ecor.at[k] for k in range(4)],
        [brow.at[0], brow.at[1], bcol.at[0], bcol.at[1]] + [bcor.at[k] for k in range(4)],
        border_s, border_r,
    )
    for copy in border:
        copy.start()
    xr[gy] = xs[gy]

    for chunk, (first, groups, start) in enumerate(CHUNKS):
        for copy in x_copies(chunk, lambda d: mod(gy - d, GY)):
            copy.wait()
        last = start + groups * 32
        rim = jnp.dot(
            edge_table[0 : groups * 64],
            xr[:, last : last + 16].reshape(128, 128),
            preferred_element_type=F32,
        )
        for pair in range(0, groups, 2):
            width = min(2, groups - pair)
            data = [
                xr[:, start + 32 * (pair + k) : start + 32 * (pair + k) + 32].reshape(256, 128)
                for k in range(width)
            ]
            c = jnp.dot(col[...], jnp.concatenate(data, axis=1), preferred_element_type=F32)
            for k in range(width):
                one = c[:, k * 128 : k * 128 + 128] + rim[(pair + k) * 64 : (pair + k) * 64 + 64]
                for part in range(2):
                    parts = [one[part * 32 + 8 * p : part * 32 + 8 * p + 8] for p in range(4)]
                    for q, block in enumerate(transpose_blocks(parts)):
                        r = part * OPEN + 4 * (first + pair + k) + q
                        half[pl.ds(r, 8, stride=2 * OPEN), :] = block
    forward_scale = 1.0 / math.sqrt(H * W)
    in_copies[1].wait()
    for pair in range(4):
        data = [
            half[(2 * pair + k) * 2 * OPEN : (2 * pair + k + 1) * 2 * OPEN].astype(BF)
            for k in range(2)
        ]
        c = jnp.dot(row[...], jnp.concatenate(data, axis=1), preferred_element_type=F32)
        c = (c * forward_scale).astype(BF)
        for k in range(2):
            for mh in range(2):
                cs[mh * 8 + 2 * pair + k] = c[mh * 64 : mh * 64 + 64, k * 128 : k * 128 + 128]
    for d in range(1, GX):
        along_x(cs.at[mod(gx + d, GX)], cr.at[gx], d, c_s.at[d], c_r.at[d]).start()
    cr[gx] = cs[gx]

    for copy in border:
        copy.wait()
    total[1] += brow[0].astype(F32) * above
    total[ROWS] += brow[1].astype(F32) * below
    own = slice(1, ROWS + 1)
    total[own, 0, :] += bcol[0].astype(F32) * left
    total[own, COLS - 1, :] += bcol[1].astype(F32) * right
    total[1, 0:1, :] += bcor[0][0:1].astype(F32) * (above * left)
    total[1, COLS - 1 : COLS, :] += bcor[1][0:1].astype(F32) * (above * right)
    total[ROWS, 0:1, :] += bcor[2][0:1].astype(F32) * (below * left)
    total[ROWS, COLS - 1 : COLS, :] += bcor[3][0:1].astype(F32) * (below * right)

    for d in range(1, GX):
        along_x(
            cs.at[mod(gx + d, GX)], cr.at[mod(gx - d, GX)], d, c_s.at[d], c_r.at[d]
        ).wait()
    coef = cr[0].astype(F32)
    for k in range(1, GX):
        coef = coef + cr[k].astype(F32)
    cg[gy] = coef.astype(BF)
    for d in range(1, GY):
        along_y(cg.at[gy], cg.at[gy], d, g_s.at[d], g_r.at[d]).start()
    in_copies[2].wait()
    in_copies[3].wait()
    for d in range(1, GY):
        along_y(cg.at[gy], cg.at[mod(gy - d, GY)], d, g_s.at[d], g_r.at[d]).wait()

    inputs = [
        transpose_blocks([cg[jt * 4 + p].astype(F32) for p in range(4)]) for jt in range(2)
    ]
    n8 = lax.rem(gx, 8)
    mh = gx // 8
    lane64 = lax.broadcasted_iota(jnp.int32, (32, KH), 1)
    row64 = lax.broadcasted_iota(jnp.int32, (32, KH), 0)
    block_of_lane = lax.broadcasted_iota(jnp.int32, (64, 512), 1) >> 5
    lane_block = lax.broadcasted_iota(jnp.int32, (64, 128), 1) >> 5
    mixer = band[...].reshape(512, CH)
    spec = jnp.zeros((64, 128), F32)
    for n4 in range(4):
        modes = jnp.concatenate([inputs[0][n4], inputs[1][n4]], axis=1).astype(BF)
        z = lax.dot_general(
            modes, mixer, (((1,), (1,)), ((), ())), preferred_element_type=F32
        )
        ids = jnp.broadcast_to(band_ids[pl.ds(4 * n8 + n4, 1), :], (32, KH))
        mine = jnp.sum(jnp.where(lane64 == row64 + 32 * mh, ids, 0), axis=1, keepdims=True)
        mine = jnp.concatenate([mine, mine], axis=0)
        z = jnp.where(block_of_lane == mine, z, 0.0)
        y = z[:, 0:128] + z[:, 128:256] + z[:, 256:384] + z[:, 384:512]
        y = y + pltpu.roll(y, 64, 1)
        y = y + pltpu.roll(y, 32, 1)
        spec = jnp.where(lane_block == n4, y, spec)
    sp[gx] = spec.astype(BF)
    for d in range(1, GX):
        along_x(sp.at[gx], sp.at[gx], d, p_s.at[d], p_r.at[d]).start()
    for d in range(1, GX):
        along_x(sp.at[gx], sp.at[mod(gx - d, GX)], d, p_s.at[d], p_r.at[d]).wait()

    inverse_scale = 1.0 / math.sqrt(2 * KH * KW)
    for pair in range(4):
        data = [
            jnp.concatenate([sp[2 * pair + k], sp[8 + 2 * pair + k]], axis=0) for k in range(2)
        ]
        z = jnp.dot(back[...], jnp.concatenate(data, axis=1), preferred_element_type=F32)
        z = z * inverse_scale
        for k in range(2):
            zs[(2 * pair + k) * 96 : (2 * pair + k + 1) * 96, :] = z[:, k * 128 : k * 128 + 128]

    def f_copies(third, target):
        rows = slice(4 * third, 4 * third + 4)
        return [
            along_y(
                fs.at[mod(gy + d, GY), rows], fr.at[target(d), rows], d,
                f_s.at[third, d], f_r.at[third, d],
            )
            for d in range(1, GY)
        ]

    for third in range(3):
        for pair in range(2 * third, 2 * third + 2):
            columns = []
            for k in range(2):
                pieces = []
                for part in range(2):
                    r = part * ROWS + 4 * (2 * pair + k)
                    parts = [zs[pl.ds(r + q, 8, stride=2 * ROWS), :] for q in range(4)]
                    pieces += list(transpose_blocks(parts))
                columns.append(jnp.concatenate(pieces, axis=0))
            data = jnp.concatenate(columns, axis=1).astype(BF)
            f = jnp.dot(col_t[...], data, preferred_element_type=F32).astype(BF)
            for k in range(2):
                for j in range(GY):
                    fs[j, 2 * pair + k] = f[j * 32 : j * 32 + 32, k * 128 : k * 128 + 128]
        for copy in f_copies(third, lambda d: gy):
            copy.start()
    fr[gy] = fs[gy]

    def join_group(g, _):
        for jt in range(2):
            lanes = slice(jt * 128, jt * 128 + 128)
            parts = [fr[jt * 4 + s, g].astype(F32) for s in range(4)]
            for q, part in enumerate(transpose_blocks(parts)):
                out[4 * g + q, :, lanes] = (total[4 * g + q + 1, :, lanes] + part).astype(BF)
        return 0

    for third in range(3):
        for copy in f_copies(third, lambda d: mod(gy - d, GY)):
            copy.wait()
        lax.fori_loop(4 * third, 4 * third + 4, join_group, 0, unroll=2)


VMEM = pl.BlockSpec(memory_space=pltpu.VMEM)
SMEM = pl.BlockSpec(memory_space=pltpu.SMEM)
ANY = pl.BlockSpec(memory_space=pl.ANY)


def dma(*shape):
    return pltpu.SemaphoreType.DMA(shape)


def border(count=1):
    one = [
        pltpu.VMEM((2, COLS, CH), BF),
        pltpu.VMEM((2, ROWS, CH), BF),
        pltpu.VMEM((4, 16, CH), BF),
    ]
    return one * count


def body(saved_mid, out_grad, expert_weight, routes, gates, band_matrix, band_ids):
    return pl.pallas_call(
        fused_body,
        name="fused",
        out_shape=jax.ShapeDtypeStruct((ROWS, COLS, CH), BF),
        in_specs=[VMEM, ANY, ANY, SMEM, SMEM, ANY, VMEM, VMEM, VMEM, VMEM, ANY, ANY],
        out_specs=VMEM,
        scratch_shapes=[
            pltpu.VMEM((ROWS, COLS, CH), BF),
            pltpu.VMEM((EXPERTS, 9 * CH, CH), BF),
            pltpu.VMEM((128, 2 * OPEN), BF),
            pltpu.VMEM((2 * ROWS, 128), BF),
            pltpu.VMEM((16, 32, CH), BF),
            pltpu.VMEM((ROWS + 2, COLS, CH), F32),
            pltpu.VMEM((3, ROWS + 2, COLS, CH), BF),
            pltpu.VMEM((2, 64, CH), F32),
            pltpu.VMEM((TILES, SLOTS, 256, CH), BF),
            pltpu.VMEM((3, OPEN, COLS, CH), F32),
            pltpu.VMEM((OPEN, COLS, CH), F32),
            pltpu.VMEM((2, 2, OPEN + 4, 128), F32),
            pltpu.VMEM((4, 2, 16, 128), F32),
            *border(4),
            pltpu.VMEM((GY, 464, 128), BF),
            pltpu.VMEM((GY, 464, 128), BF),
            pltpu.VMEM((8 * 2 * OPEN, 128), F32),
            pltpu.VMEM((GX, 64, 128), BF),
            pltpu.VMEM((GX, 64, 128), BF),
            pltpu.VMEM((GY, 64, 128), BF),
            pltpu.VMEM((GX, 64, 128), BF),
            pltpu.VMEM((8 * 2 * ROWS, 128), F32),
            pltpu.VMEM((GY, 12, 32, 128), BF),
            pltpu.VMEM((GY, 12, 32, 128), BF),
            dma(EXPERTS), dma(4), dma(8), dma(8), dma(8), dma(8),
            dma(3, GY), dma(3, GY), dma(GX), dma(GX), dma(GY), dma(GY),
            dma(GX), dma(GX), dma(3, GY), dma(3, GY),
        ],
        compiler_params=pltpu.CompilerParams(
            collective_id=0, has_side_effects=True, vmem_limit_bytes=60 * 2**20
        ),
    )(
        saved_mid, out_grad, expert_weight.reshape(EXPERTS, 9 * CH, CH), routes, gates,
        band_matrix, band_ids.T, jnp.asarray(COL_TABLE, BF), jnp.asarray(COL_TABLE.T, BF),
        jnp.asarray(EDGE_TABLE, BF), jnp.asarray(ROW_TABLE, BF), jnp.asarray(BACK_TABLE, BF),
    )


def solution(mesh):
    placed = (
        P("gx", "gy", None),
        P("gx", "gy", None),
        P(),
        P("gx", "gy", None),
        P("gx", "gy", None),
        P(),
        P(),
    )
    return jax.shard_map(
        body, mesh=mesh, in_specs=placed, out_specs=P("gx", "gy", None), check_vma=False
    )
```

time: 113 us -> 84.6 us (0.75); the launches traced: 112 us -> 84.4 us
  Pallas kernels: 109 us -> 82.3 us
    pallas_call x3 -> x1, Pallas kernels: 109 us -> 82.3 us  [body(): pl.pallas_call(fused_body, name='fused', out_shape=jax.ShapeDtypeStruct((...]
    unnamed x4 -> x1, local copies, waits for them, and re-layouts: 2.77 us -> 2.06 us
where the time goes in v2:
time: 84.6 us; the launch traced here: 84.4 us
  Pallas kernels  82.3 us (97%)
  local copies, waits for them, and re-layouts  2.06 us (2%)
    pallas_call x1, Pallas kernels, body(): pl.pallas_call(fused_body, name='fused', out_shape=jax.ShapeDtypeStruct((...  82.3 us
    unnamed x1, local copies, waits for them, and re-layouts  2.06 us

profile of v2, /device:TPU:0, one launch (start us, length us, event | category | flops | bytes accessed | tf_op | source)
XLA Modules:
  0.0 84.4 jit_solution(997087527647788100)
XLA Ops:
  0.0 82.3 %fused.1 = bf16[48,32,256]{2,1,0:T(8,128)(2,1)} custom-call(bf16[48,32,256]{2,1,0:T(8,128)(2,1)} %mid.1, bf16[48,32,256]{2,1,0:T(8,128)(2,1)} %grad_hbm.1, bf16[10,2304,256]{2,1,0:T(8,128)(2,1)} %bitcast.2, s32[3,2,4]{2,1,0:T(2,128)} %routes.1, f32[3,2,6]{2,1,0:T(2,128)} %gates.1, bf16[16,256,256]{2,1,0:T(8,128)(2,1)} %band_hbm.1, s32[32,64]{1,0:T(8,128)} %bitcast.3, ...), custom_call_target="tpu_custom_call" | custom-call | tf_op jit(solution)/shard_map/fused/pallas_call | solution.py:480
  82.3 2.1 %copy.14 = bf16[48,32,256]{2,1,0:T(8,128)(2,1)} copy(bf16[48,32,256]{2,1,0:T(8,128)(2,1)} %fused.1) | data formatting | bytes 1572864

commit v3 on v2

--- a/solution.py
+++ b/solution.py
@@ -33,11 +33,14 @@
         theta = 2 * np.pi * ((n[:, None] * columns[None, :]) % W) / W
         return np.concatenate([np.cos(theta), np.sin(theta)])
 
-    col = wave(np.arange(W))
+    opened = np.zeros((64, 2, GY, 16))
     edge = np.zeros((5, 64, GY, 16))
     for j in range(GY):
-        for side, column in enumerate((COLS * j - 1, COLS * j + COLS)):
-            if 0 <= column < W:
+        for part in range(2):
+            columns = COLS * j + 16 * part - 1 + np.arange(16)
+            opened[:, part, j] = wave(columns) * (columns >= 0)
+        for side, column in enumerate((COLS * j + COLS - 1, COLS * j + COLS)):
+            if column < W:
                 for g in range(5):
                     edge[g, :, j, side * 8 + g] = wave(np.array([column]))[:, 0]
     m = np.arange(KH)
@@ -52,10 +55,11 @@
         row[gx, :, 0, :, 0], row[gx, :, 0, :, 1] = rc, -rs
         row[gx, :, 1, :, 0], row[gx, :, 1, :, 1] = rs, rc
     back = row[..., 1 : ROWS + 1].reshape(GX, 128, 2 * ROWS).transpose(0, 2, 1)
-    return col, edge.reshape(320, 128), row.reshape(GX, 128, 2 * OPEN), back
-
-
-COL_TABLE, EDGE_TABLE, ROW_TABLE, BACK_TABLE = tables()
+    row = row.reshape(GX, 128, 2 * OPEN)
+    return opened.reshape(64, 256), wave(np.arange(W)).T, edge.reshape(320, 128), row, back
+
+
+OPEN_TABLE, COL_TABLE, EDGE_TABLE, ROW_TABLE, BACK_TABLE = tables()
 
 
 def gelu_slope_twice(values):
@@ -105,9 +109,10 @@
 
 
 def fused_body(
-    mid, grad_hbm, w_hbm, routes, gates, band_hbm, band_ids, col, col_t, edge_table, row_hbm, back_hbm,
+    mid_hbm, grad_hbm, w_hbm, routes, gates, band_hbm, band_ids,
+    col_hbm, col_t_hbm, edge_hbm, row_hbm, back_hbm,
     out,
-    grad, w, row, back, band, ext, shifted, side, deltas, spread, total, edge, edges,
+    mid, grad, w, row, back, band, col, col_t, edge_table, ext, shifted, side, deltas, spread, total, edge, edges, left_edge,
     erow, ecol, ecor, rrow, rcol, rcor, brow, bcol, bcor, hrow, hcol, hcor,
     xs, xr, half, cs, cr, cg, sp, zs, fs, fr,
     w_sem, in_sem, halo_s, halo_r, border_s, border_r,
@@ -115,17 +120,17 @@
 ):
     gx, gy = lax.axis_index("gx"), lax.axis_index("gy")
     w_copies = [pltpu.make_async_copy(w_hbm.at[e], w.at[e], w_sem.at[e]) for e in range(EXPERTS)]
+    sources = [
+        mid_hbm, grad_hbm, row_hbm.at[gx], back_hbm.at[gx],
+        band_hbm.at[:, pl.ds(pl.multiple_of(gy * 32, 32), 32), :],
+        col_hbm, col_t_hbm, edge_hbm,
+    ]
+    targets = [mid, grad, row, back, band, col, col_t, edge_table]
     in_copies = [
-        pltpu.make_async_copy(grad_hbm, grad, in_sem.at[0]),
-        pltpu.make_async_copy(row_hbm.at[gx], row, in_sem.at[1]),
-        pltpu.make_async_copy(back_hbm.at[gx], back, in_sem.at[2]),
-        pltpu.make_async_copy(
-            band_hbm.at[:, pl.ds(pl.multiple_of(gy * 32, 32), 32), :], band, in_sem.at[3]
-        ),
+        pltpu.make_async_copy(source, target, in_sem.at[k])
+        for k, (source, target) in enumerate(zip(sources, targets))
     ]
-    w_copies[0].start()
-    in_copies[0].start()
-    for copy in w_copies[1:] + in_copies[1:]:
+    for copy in in_copies[:1] + w_copies[:1] + in_copies[1:2] + w_copies[1:] + in_copies[2:]:
         copy.start()
     barrier = pltpu.get_barrier_semaphore()
     partners = [(gx, mod(gy + d, GY)) for d in range(1, GY)]
@@ -139,6 +144,7 @@
     left = jnp.where(gy > 0, 1.0, 0.0)
     right = jnp.where(gy < GY - 1, 1.0, 0.0)
 
+    in_copies[0].wait()
     ext[1 : ROWS + 1] = mid[...].astype(F32)
     hcol[0] = ext[1 : ROWS + 1, COLS - 1, :].astype(BF)
     hcol[1] = ext[1 : ROWS + 1, 0, :].astype(BF)
@@ -153,7 +159,12 @@
     )
     for copy in halo:
         copy.start()
-    spread[...] = jnp.zeros_like(spread)
+    in_copies[1].wait()
+    for b in (0, 2):
+        spread[b] = jnp.zeros((OPEN, COLS, CH), F32)
+    spread[1, 0] = jnp.zeros((COLS, CH), F32)
+    spread[1, 1 : ROWS + 1] = grad[...].astype(F32)
+    spread[1, ROWS + 1 :] = jnp.zeros((OPEN - ROWS - 1, COLS, CH), F32)
     edges[...] = jnp.zeros_like(edges)
     for copy in halo:
         copy.wait()
@@ -204,7 +215,6 @@
         forward(s, expert)
         return 0
 
-    in_copies[0].wait()
     w_copies[0].wait()
     w_copies[1].wait()
     lax.fori_loop(0, 2, forward_shared, 0)
@@ -224,8 +234,8 @@
             device_id=(mod(gx + d, GX), gy), device_id_type=MESH,
         )
 
-    def backward(t, _):
-        rt, cols = t // 2, pl.ds(pl.multiple_of((t % 2) * 16, 16), 16)
+    def backward(t):
+        rt, cols = t // 2, slice((t % 2) * 16, (t % 2) * 16 + 16)
         d = jnp.concatenate([deltas[t, s] for s in range(SLOTS)], axis=1)
         chosen = [0, 1] + [expert(t, s) for s in range(2, SLOTS)]
         for a in range(3):
@@ -237,68 +247,81 @@
                 r = lax.dot_general(
                     d, kernels, (((1,), (1,)), ((), ())), preferred_element_type=F32
                 )
-                spread[b, pl.ds(rt * 16 + a, 16), cols, :] += r.reshape(16, 16, CH)
-        return 0
-
-    def joined(r):
-        ahead = jnp.where(place > 0, pltpu.roll(spread[2, r], 1, 0), 0.0)
-        behind = jnp.where(place < COLS - 1, pltpu.roll(spread[0, r], COLS - 1, 0), 0.0)
-        return spread[1, r] + ahead + behind
-
-    def x_copies(chunk, target):
-        _, groups, start = CHUNKS[chunk]
-        rows = slice(start, start + groups * 32 + 16)
+                spread[b, rt * 16 + a : rt * 16 + a + 16, cols, :] += r.reshape(16, 16, CH)
+
+    def x_copies(t, target):
+        _, groups, start = CHUNKS[t // 2]
+        rows = slice(start, start + groups * 16)
+        if t % 2:
+            rows = slice(start + groups * 16, start + groups * 32 + 16)
         return [
             along_y(
                 xs.at[mod(gy + d, GY), rows], xr.at[target(d), rows], d,
-                x_s.at[chunk, d], x_r.at[chunk, d],
+                x_s.at[t, d], x_r.at[t, d],
             )
             for d in range(1, GY)
         ]
 
-    for chunk, (first, groups, start) in enumerate(CHUNKS):
-        lax.fori_loop(2 * chunk, 2 * chunk + 2, backward, 0)
+    place16 = lax.broadcasted_iota(jnp.int32, (16, CH), 0)
+    for t in range(TILES):
+        backward(t)
+        first, groups, start = CHUNKS[t // 2]
+        base = start + (t % 2) * groups * 16
+
+        def opened(r):
+            if t % 2 == 0:
+                middle = jnp.where(place16 >= 1, pltpu.roll(spread[1, r, 0:16, :], 1, 0), 0.0)
+                ahead = jnp.where(place16 >= 2, pltpu.roll(spread[2, r, 0:16, :], 2, 0), 0.0)
+                return spread[0, r, 0:16, :] + middle + ahead
+            middle = pltpu.roll(spread[1, r, 8:32, :], 1, 0)[8:24]
+            ahead = pltpu.roll(spread[2, r, 8:32, :], 2, 0)[8:24]
+            return spread[0, r, 16:32, :] + middle + ahead
 
         def split_group(k, _):
-            g = first + k
-            for q in range(4):
-                r = 4 * g + q
-                keep = jnp.where((r >= 1) & (r <= ROWS), 1.0, 0.0)
-                field = grad[jnp.clip(r - 1, 0, ROWS - 1)].astype(F32)
-                total[r] = joined(r) + field * keep
+            lines = [opened(4 * (first + k) + q) for q in range(4)]
             for jt in range(2):
                 lanes = slice(jt * 128, jt * 128 + 128)
-                parts = [total[4 * g + q, :, lanes] for q in range(4)]
-                for s, part in enumerate(transpose_blocks(parts)):
-                    rows = pl.ds(pl.multiple_of(start + 32 * k, 16), 32)
-                    xs[jt * 4 + s, rows, :] = part.astype(BF)
+                for s, part in enumerate(transpose_blocks([line[:, lanes] for line in lines])):
+                    xs[jt * 4 + s, pl.ds(pl.multiple_of(base + 16 * k, 16), 16), :] = part.astype(BF)
             return 0
 
-        lax.fori_loop(0, groups, split_group, 0)
-        rows = slice(4 * first, 4 * first + 4 * groups)
-        for jt in range(2):
-            lanes = slice(jt * 128, jt * 128 + 128)
-            edge[0, jt, rows] = spread[0, rows, 0, lanes]
-            edge[1, jt, rows] = spread[2, rows, COLS - 1, lanes]
-            for q in range(4):
-                for s in range(2):
-                    edges[q, jt, s * 8 : s * 8 + groups] = edge[
-                        s, jt, pl.ds(4 * first + q, groups, stride=4), :
-                    ]
-            for s, part in enumerate(transpose_blocks([edges[q, jt] for q in range(4)])):
-                last = start + groups * 32
-                xs[jt * 4 + s, last : last + 16, :] = part.astype(BF)
-        for copy in x_copies(chunk, lambda d: gy):
+        lax.fori_loop(0, groups, split_group, 0, unroll=groups)
+        if t % 2:
+            rows = slice(4 * first, 4 * first + 4 * groups)
+            last = start + groups * 32
+            for jt in range(2):
+                lanes = slice(jt * 128, jt * 128 + 128)
+                edge[0, jt, rows] = (
+                    spread[1, rows, COLS - 1, lanes] + spread[2, rows, COLS - 2, lanes]
+                )
+                edge[1, jt, rows] = spread[2, rows, COLS - 1, lanes]
+                for q in range(4):
+                    for s in range(2):
+                        edges[q, jt, s * 8 : s * 8 + groups] = edge[
+                            s, jt, pl.ds(4 * first + q, groups, stride=4), :
+                        ]
+                for s, part in enumerate(transpose_blocks([edges[q, jt] for q in range(4)])):
+                    xs[jt * 4 + s, last : last + 16, :] = part.astype(BF)
+        for copy in x_copies(t, lambda d: gy):
             copy.start()
 
+    def own_row(r, _):
+        ahead = jnp.where(place > 0, pltpu.roll(spread[2, r], 1, 0), 0.0)
+        behind = jnp.where(place < COLS - 1, pltpu.roll(spread[0, r], COLS - 1, 0), 0.0)
+        total[r] = spread[1, r] + ahead + behind
+        return 0
+
+    lax.fori_loop(0, ROWS + 2, own_row, 0, unroll=5)
     erow[0] = total[ROWS + 1].astype(BF)
     erow[1] = total[0].astype(BF)
     for jt in range(2):
         lanes = slice(jt * 128, jt * 128 + 128)
+        left_edge[jt, 0 : ROWS + 2] = spread[0, 0 : ROWS + 2, 0, lanes]
         ecol[0, :, lanes] = edge[1, jt, 1 : ROWS + 1].astype(BF)
-        ecol[1, :, lanes] = edge[0, jt, 1 : ROWS + 1].astype(BF)
-        for k, (s, r) in enumerate(((1, ROWS + 1), (0, ROWS + 1), (1, 0), (0, 0))):
-            ecor[k, :, lanes] = jnp.broadcast_to(edge[s, jt, r : r + 1, :], (16, 128)).astype(BF)
+        ecol[1, :, lanes] = left_edge[jt, 1 : ROWS + 1].astype(BF)
+        for k, r in enumerate((ROWS + 1, ROWS + 1, 0, 0)):
+            corner = left_edge[jt, r : r + 1, :] if k % 2 else edge[1, jt, r : r + 1, :]
+            ecor[k, :, lanes] = jnp.broadcast_to(corner, (16, 128)).astype(BF)
     border = border_copies(
         gx, gy,
         [erow.at[0], erow.at[1], ecol.at[0], ecol.at[1]] + [ecor.at[k] for k in range(4)],
@@ -309,8 +332,12 @@
         copy.start()
     xr[gy] = xs[gy]
 
+    for copy in in_copies[2:]:
+        copy.wait()
     for chunk, (first, groups, start) in enumerate(CHUNKS):
-        for copy in x_copies(chunk, lambda d: mod(gy - d, GY)):
+        for copy in x_copies(2 * chunk, lambda d: mod(gy - d, GY)):
+            copy.wait()
+        for copy in x_copies(2 * chunk + 1, lambda d: mod(gy - d, GY)):
             copy.wait()
         last = start + groups * 32
         rim = jnp.dot(
@@ -320,10 +347,11 @@
         )
         for pair in range(0, groups, 2):
             width = min(2, groups - pair)
-            data = [
-                xr[:, start + 32 * (pair + k) : start + 32 * (pair + k) + 32].reshape(256, 128)
-                for k in range(width)
-            ]
+            data = []
+            for k in range(pair, pair + width):
+                halves = [start + 16 * (groups * part + k) for part in range(2)]
+                halves = [xr[:, at : at + 16].reshape(128, 128) for at in halves]
+                data.append(jnp.concatenate(halves, axis=0))
             c = jnp.dot(col[...], jnp.concatenate(data, axis=1), preferred_element_type=F32)
             for k in range(width):
                 one = c[:, k * 128 : k * 128 + 128] + rim[(pair + k) * 64 : (pair + k) * 64 + 64]
@@ -333,7 +361,6 @@
                         r = part * OPEN + 4 * (first + pair + k) + q
                         half[pl.ds(r, 8, stride=2 * OPEN), :] = block
     forward_scale = 1.0 / math.sqrt(H * W)
-    in_copies[1].wait()
     for pair in range(4):
         data = [
             half[(2 * pair + k) * 2 * OPEN : (2 * pair + k + 1) * 2 * OPEN].astype(BF)
@@ -344,8 +371,25 @@
         for k in range(2):
             for mh in range(2):
                 cs[mh * 8 + 2 * pair + k] = c[mh * 64 : mh * 64 + 64, k * 128 : k * 128 + 128]
-    for d in range(1, GX):
-        along_x(cs.at[mod(gx + d, GX)], cr.at[gx], d, c_s.at[d], c_r.at[d]).start()
+    parts_of = [slice(0, 32), slice(32, 64)]
+
+    def c_copy(part, d, target):
+        rows = parts_of[part]
+        return along_x(
+            cs.at[mod(gx + d, GX), rows], cr.at[target, rows], d, c_s.at[part, d], c_r.at[part, d]
+        )
+
+    def g_copy(part, d, target):
+        rows = parts_of[part]
+        return along_y(cg.at[gy, rows], cg.at[target, rows], d, g_s.at[part, d], g_r.at[part, d])
+
+    def p_copy(part, d, target):
+        rows = parts_of[part]
+        return along_x(sp.at[gx, rows], sp.at[target, rows], d, p_s.at[part, d], p_r.at[part, d])
+
+    for part in range(2):
+        for d in range(1, GX):
+            c_copy(part, d, gx).start()
     cr[gx] = cs[gx]
 
     for copy in border:
@@ -360,50 +404,57 @@
     total[ROWS, 0:1, :] += bcor[2][0:1].astype(F32) * (below * left)
     total[ROWS, COLS - 1 : COLS, :] += bcor[3][0:1].astype(F32) * (below * right)
 
-    for d in range(1, GX):
-        along_x(
-            cs.at[mod(gx + d, GX)], cr.at[mod(gx - d, GX)], d, c_s.at[d], c_r.at[d]
-        ).wait()
-    coef = cr[0].astype(F32)
-    for k in range(1, GX):
-        coef = coef + cr[k].astype(F32)
-    cg[gy] = coef.astype(BF)
-    for d in range(1, GY):
-        along_y(cg.at[gy], cg.at[gy], d, g_s.at[d], g_r.at[d]).start()
-    in_copies[2].wait()
-    in_copies[3].wait()
-    for d in range(1, GY):
-        along_y(cg.at[gy], cg.at[mod(gy - d, GY)], d, g_s.at[d], g_r.at[d]).wait()
-
-    inputs = [
-        transpose_blocks([cg[jt * 4 + p].astype(F32) for p in range(4)]) for jt in range(2)
-    ]
     n8 = lax.rem(gx, 8)
     mh = gx // 8
     lane64 = lax.broadcasted_iota(jnp.int32, (32, KH), 1)
     row64 = lax.broadcasted_iota(jnp.int32, (32, KH), 0)
-    block_of_lane = lax.broadcasted_iota(jnp.int32, (64, 512), 1) >> 5
-    lane_block = lax.broadcasted_iota(jnp.int32, (64, 128), 1) >> 5
+    block_of_lane = lax.broadcasted_iota(jnp.int32, (32, 512), 1) >> 5
+    lane_block = lax.broadcasted_iota(jnp.int32, (32, 128), 1) >> 5
+    band_of = []
+    for n4 in range(4):
+        ids = jnp.broadcast_to(band_ids[pl.ds(4 * n8 + n4, 1), :], (32, KH))
+        band_of.append(jnp.sum(jnp.where(lane64 == row64 + 32 * mh, ids, 0), axis=1, keepdims=True))
+
+    for part in range(2):
+        rows = parts_of[part]
+        for d in range(1, GX):
+            c_copy(part, d, mod(gx - d, GX)).wait()
+        coef = cr[0, rows].astype(F32)
+        for k in range(1, GX):
+            coef = coef + cr[k, rows].astype(F32)
+        cg[gy, rows] = coef.astype(BF)
+        for d in range(1, GY):
+            g_copy(part, d, gy).start()
+
     mixer = band[...].reshape(512, CH)
-    spec = jnp.zeros((64, 128), F32)
-    for n4 in range(4):
-        modes = jnp.concatenate([inputs[0][n4], inputs[1][n4]], axis=1).astype(BF)
-        z = lax.dot_general(
-            modes, mixer, (((1,), (1,)), ((), ())), preferred_element_type=F32
+    for part in range(2):
+        rows = parts_of[part]
+        for d in range(1, GY):
+            g_copy(part, d, mod(gy - d, GY)).wait()
+        inputs = [
+            transpose_blocks([cg[jt * 4 + p, rows].astype(F32) for p in range(4)])
+            for jt in range(2)
+        ]
+        spec = jnp.zeros((32, 128), F32)
+        modes = [
+            jnp.concatenate([inputs[0][n4], inputs[1][n4]], axis=1).astype(BF) for n4 in range(4)
+        ]
+        mixed = lax.dot_general(
+            jnp.concatenate(modes, axis=0), mixer, (((1,), (1,)), ((), ())),
+            preferred_element_type=F32,
         )
-        ids = jnp.broadcast_to(band_ids[pl.ds(4 * n8 + n4, 1), :], (32, KH))
-        mine = jnp.sum(jnp.where(lane64 == row64 + 32 * mh, ids, 0), axis=1, keepdims=True)
-        mine = jnp.concatenate([mine, mine], axis=0)
-        z = jnp.where(block_of_lane == mine, z, 0.0)
-        y = z[:, 0:128] + z[:, 128:256] + z[:, 256:384] + z[:, 384:512]
-        y = y + pltpu.roll(y, 64, 1)
-        y = y + pltpu.roll(y, 32, 1)
-        spec = jnp.where(lane_block == n4, y, spec)
-    sp[gx] = spec.astype(BF)
-    for d in range(1, GX):
-        along_x(sp.at[gx], sp.at[gx], d, p_s.at[d], p_r.at[d]).start()
-    for d in range(1, GX):
-        along_x(sp.at[gx], sp.at[mod(gx - d, GX)], d, p_s.at[d], p_r.at[d]).wait()
+        for n4 in range(4):
+            z = jnp.where(block_of_lane == band_of[n4], mixed[n4 * 32 : n4 * 32 + 32], 0.0)
+            y = z[:, 0:128] + z[:, 128:256] + z[:, 256:384] + z[:, 384:512]
+            y = y + pltpu.roll(y, 64, 1)
+            y = y + pltpu.roll(y, 32, 1)
+            spec = jnp.where(lane_block == n4, y, spec)
+        sp[gx, rows] = spec.astype(BF)
+        for d in range(1, GX):
+            p_copy(part, d, gx).start()
+    for part in range(2):
+        for d in range(1, GX):
+            p_copy(part, d, mod(gx - d, GX)).wait()
 
     inverse_scale = 1.0 / math.sqrt(2 * KH * KW)
     for pair in range(4):
@@ -480,15 +531,19 @@
     return pl.pallas_call(
         fused_body,
         name="fused",
-        out_shape=jax.ShapeDtypeStruct((ROWS, COLS, CH), BF),
-        in_specs=[VMEM, ANY, ANY, SMEM, SMEM, ANY, VMEM, VMEM, VMEM, VMEM, ANY, ANY],
+        out_shape=pltpu.VMEM((ROWS, COLS, CH), BF),
+        in_specs=[ANY, ANY, ANY, SMEM, SMEM, ANY, VMEM, ANY, ANY, ANY, ANY, ANY],
         out_specs=VMEM,
         scratch_shapes=[
+            pltpu.VMEM((ROWS, COLS, CH), BF),
             pltpu.VMEM((ROWS, COLS, CH), BF),
             pltpu.VMEM((EXPERTS, 9 * CH, CH), BF),
             pltpu.VMEM((128, 2 * OPEN), BF),
             pltpu.VMEM((2 * ROWS, 128), BF),
             pltpu.VMEM((16, 32, CH), BF),
+            pltpu.VMEM((64, 256), BF),
+            pltpu.VMEM((256, 64), BF),
+            pltpu.VMEM((320, 128), BF),
             pltpu.VMEM((ROWS + 2, COLS, CH), F32),
             pltpu.VMEM((3, ROWS + 2, COLS, CH), BF),
             pltpu.VMEM((2, 64, CH), F32),
@@ -497,6 +552,7 @@
             pltpu.VMEM((OPEN, COLS, CH), F32),
             pltpu.VMEM((2, 2, OPEN + 4, 128), F32),
             pltpu.VMEM((4, 2, 16, 128), F32),
+            pltpu.VMEM((2, OPEN + 4, 128), F32),
             *border(4),
             pltpu.VMEM((GY, 464, 128), BF),
             pltpu.VMEM((GY, 464, 128), BF),
@@ -508,16 +564,16 @@
             pltpu.VMEM((8 * 2 * ROWS, 128), F32),
             pltpu.VMEM((GY, 12, 32, 128), BF),
             pltpu.VMEM((GY, 12, 32, 128), BF),
-            dma(EXPERTS), dma(4), dma(8), dma(8), dma(8), dma(8),
-            dma(3, GY), dma(3, GY), dma(GX), dma(GX), dma(GY), dma(GY),
-            dma(GX), dma(GX), dma(3, GY), dma(3, GY),
+            dma(EXPERTS), dma(8), dma(8), dma(8), dma(8), dma(8),
+            dma(6, GY), dma(6, GY), dma(2, GX), dma(2, GX), dma(2, GY), dma(2, GY),
+            dma(2, GX), dma(2, GX), dma(3, GY), dma(3, GY),
         ],
         compiler_params=pltpu.CompilerParams(
-            collective_id=0, has_side_effects=True, vmem_limit_bytes=60 * 2**20
+            collective_id=0, has_side_effects=True, vmem_limit_bytes=66_000_000
         ),
     )(
         saved_mid, out_grad, expert_weight.reshape(EXPERTS, 9 * CH, CH), routes, gates,
-        band_matrix, band_ids.T, jnp.asarray(COL_TABLE, BF), jnp.asarray(COL_TABLE.T, BF),
+        band_matrix, band_ids.T, jnp.asarray(OPEN_TABLE, BF), jnp.asarray(COL_TABLE, BF),
         jnp.asarray(EDGE_TABLE, BF), jnp.asarray(ROW_TABLE, BF), jnp.asarray(BACK_TABLE, BF),
     )
 

time: 84.6 us -> 89 us (1.052)
  Pallas kernels: 82.3 us -> 87.9 us
  local copies, waits for them, and re-layouts: 2.06 us -> 0.88 us
    pallas_call x1, Pallas kernels: 82.3 us -> 87.9 us  [body(): pl.pallas_call(fused_body, name='fused', out_shape=pltpu.VMEM((ROWS, COLS...]
    unnamed x1, local copies, waits for them, and re-layouts: 2.06 us -> 0.88 us
where the time goes in v3:
time: 89 us; the launch traced here: 88.8 us
  Pallas kernels  87.9 us (99%)
    pallas_call x1, Pallas kernels, body(): pl.pallas_call(fused_body, name='fused', out_shape=pltpu.VMEM((ROWS, COLS...  87.9 us

profile of v3, /device:TPU:0, one launch (start us, length us, event | category | flops | bytes accessed | tf_op | source)
XLA Modules:
  0.0 88.8 jit_solution(15402837423783541084)
XLA Ops:
  0.0 87.9 %fused.1 = bf16[48,32,256]{2,1,0:T(8,128)(2,1)S(1)} custom-call(bf16[48,32,256]{2,1,0:T(8,128)(2,1)} %mid_hbm.1, bf16[48,32,256]{2,1,0:T(8,128)(2,1)} %grad_hbm.1, bf16[10,2304,256]{2,1,0:T(8,128)(2,1)} %bitcast.2, s32[3,2,4]{2,1,0:T(2,128)} %routes.1, f32[3,2,6]{2,1,0:T(2,128)} %gates.1, bf16[16,256,256]{2,1,0:T(8,128)(2,1)} %band_hbm.1, s32[32,64]{1,0:T(8,128)} %bitcast.3, ...), custom_call_target="tpu_custom_call" | custom-call | tf_op jit(solution)/shard_map/fused/pallas_call | solution.py:531
  87.9 0.9 copy.14

commit v4 on v3

--- a/solution.py
+++ b/solution.py
@@ -20,6 +20,7 @@
 CHUNKS = ((0, 4, 0), (4, 4, 144), (8, 5, 288))
 
 DIRS = ((1, 0), (-1, 0), (0, 1), (0, -1), (1, 1), (1, -1), (-1, 1), (-1, -1))
+PARTS = ((0, 32), (32, 64), (64, 112), (112, 160), (160, 176), (176, 192), (192, 208), (208, 224))
 
 
 def mod(value, count):
@@ -92,20 +93,27 @@
     return a, b, c, d
 
 
-def border_copies(gx, gy, sources, targets, send_sem, recv_sem):
-    copies = []
-    for k, (dr, dc) in enumerate(DIRS):
-        copies.append(
-            pltpu.make_async_remote_copy(
-                src_ref=sources[k],
-                dst_ref=targets[k],
-                send_sem=send_sem.at[k],
-                recv_sem=recv_sem.at[k],
-                device_id=(mod(gx + dr, GX), mod(gy + dc, GY)),
-                device_id_type=MESH,
-            )
+def border_copies(gx, gy, source, target, send_sem, recv_sem):
+    copies = [
+        pltpu.make_async_remote_copy(
+            src_ref=source.at[first:last],
+            dst_ref=target.at[first:last],
+            send_sem=send_sem,
+            recv_sem=recv_sem,
+            device_id=(mod(gx + dr, GX), mod(gy + dc, GY)),
+            device_id_type=MESH,
         )
-    return copies
+        for (dr, dc), (first, last) in zip(DIRS, PARTS)
+    ]
+    whole = pltpu.make_async_remote_copy(
+        src_ref=source,
+        dst_ref=target,
+        send_sem=send_sem,
+        recv_sem=recv_sem,
+        device_id=(mod(gx + 1, GX), gy),
+        device_id_type=MESH,
+    )
+    return copies, whole
 
 
 def fused_body(
@@ -113,13 +121,16 @@
     col_hbm, col_t_hbm, edge_hbm, row_hbm, back_hbm,
     out,
     mid, grad, w, row, back, band, col, col_t, edge_table, ext, shifted, side, deltas, spread, total, edge, edges, left_edge,
-    erow, ecol, ecor, rrow, rcol, rcor, brow, bcol, bcor, hrow, hcol, hcor,
+    border_out, border_in, halo_out, halo_in,
     xs, xr, half, cs, cr, cg, sp, zs, fs, fr,
     w_sem, in_sem, halo_s, halo_r, border_s, border_r,
     x_s, x_r, c_s, c_r, g_s, g_r, p_s, p_r, f_s, f_r,
 ):
     gx, gy = lax.axis_index("gx"), lax.axis_index("gy")
-    w_copies = [pltpu.make_async_copy(w_hbm.at[e], w.at[e], w_sem.at[e]) for e in range(EXPERTS)]
+    w_copies = [
+        pltpu.make_async_copy(w_hbm.at[first:last], w.at[first:last], w_sem.at[k])
+        for k, (first, last) in enumerate(((0, 1), (1, 2), (2, EXPERTS)))
+    ]
     sources = [
         mid_hbm, grad_hbm, row_hbm.at[gx], back_hbm.at[gx],
         band_hbm.at[:, pl.ds(pl.multiple_of(gy * 32, 32), 32), :],
@@ -146,17 +157,15 @@
 
     in_copies[0].wait()
     ext[1 : ROWS + 1] = mid[...].astype(F32)
-    hcol[0] = ext[1 : ROWS + 1, COLS - 1, :].astype(BF)
-    hcol[1] = ext[1 : ROWS + 1, 0, :].astype(BF)
+    halo_out[0:32] = mid[ROWS - 1]
+    halo_out[32:64] = mid[0]
+    halo_out[64:112] = ext[1 : ROWS + 1, COLS - 1, :].astype(BF)
+    halo_out[112:160] = ext[1 : ROWS + 1, 0, :].astype(BF)
     for k, (r, c) in enumerate(((ROWS, COLS - 1), (ROWS, 0), (1, COLS - 1), (1, 0))):
-        hcor[k] = jnp.broadcast_to(ext[r, c : c + 1, :], (16, CH)).astype(BF)
+        corner = jnp.broadcast_to(ext[r, c : c + 1, :], (16, CH)).astype(BF)
+        halo_out[160 + 16 * k : 176 + 16 * k] = corner
     pl.semaphore_wait(barrier, len(partners))
-    halo = border_copies(
-        gx, gy,
-        [mid.at[ROWS - 1], mid.at[0], hcol.at[0], hcol.at[1]] + [hcor.at[k] for k in range(4)],
-        [rrow.at[0], rrow.at[1], rcol.at[0], rcol.at[1]] + [rcor.at[k] for k in range(4)],
-        halo_s, halo_r,
-    )
+    halo, halo_all = border_copies(gx, gy, halo_out, halo_in, halo_s.at[0], halo_r.at[0])
     for copy in halo:
         copy.start()
     in_copies[1].wait()
@@ -166,16 +175,15 @@
     spread[1, 1 : ROWS + 1] = grad[...].astype(F32)
     spread[1, ROWS + 1 :] = jnp.zeros((OPEN - ROWS - 1, COLS, CH), F32)
     edges[...] = jnp.zeros_like(edges)
-    for copy in halo:
-        copy.wait()
-    ext[0] = rrow[0].astype(F32) * above
-    ext[ROWS + 1] = rrow[1].astype(F32) * below
-    side[0, 8 : 8 + ROWS] = rcol[0].astype(F32) * left
-    side[1, 8 : 8 + ROWS] = rcol[1].astype(F32) * right
-    side[0, 7:8] = rcor[0][0:1].astype(F32) * (above * left)
-    side[1, 7:8] = rcor[1][0:1].astype(F32) * (above * right)
-    side[0, 8 + ROWS : 9 + ROWS] = rcor[2][0:1].astype(F32) * (below * left)
-    side[1, 8 + ROWS : 9 + ROWS] = rcor[3][0:1].astype(F32) * (below * right)
+    halo_all.wait()
+    ext[0] = halo_in[0:32].astype(F32) * above
+    ext[ROWS + 1] = halo_in[32:64].astype(F32) * below
+    side[0, 8 : 8 + ROWS] = halo_in[64:112].astype(F32) * left
+    side[1, 8 : 8 + ROWS] = halo_in[112:160].astype(F32) * right
+    side[0, 7:8] = halo_in[160:176].astype(F32)[0:1] * (above * left)
+    side[1, 7:8] = halo_in[176:192].astype(F32)[0:1] * (above * right)
+    side[0, 8 + ROWS : 9 + ROWS] = halo_in[192:208].astype(F32)[0:1] * (below * left)
+    side[1, 8 + ROWS : 9 + ROWS] = halo_in[208:224].astype(F32)[0:1] * (below * right)
     place = lax.broadcasted_iota(jnp.int32, (COLS, CH), 0)
 
     def shift_row(r, _):
@@ -218,8 +226,7 @@
     w_copies[0].wait()
     w_copies[1].wait()
     lax.fori_loop(0, 2, forward_shared, 0)
-    for copy in w_copies[2:]:
-        copy.wait()
+    w_copies[2].wait()
     lax.fori_loop(2, SLOTS, forward_routed, 0)
 
     def along_y(source, target, d, send, recv):
@@ -234,51 +241,28 @@
             device_id=(mod(gx + d, GX), gy), device_id_type=MESH,
         )
 
-    def backward(t):
-        rt, cols = t // 2, slice((t % 2) * 16, (t % 2) * 16 + 16)
-        d = jnp.concatenate([deltas[t, s] for s in range(SLOTS)], axis=1)
-        chosen = [0, 1] + [expert(t, s) for s in range(2, SLOTS)]
-        for a in range(3):
-            for b in range(3):
-                tap = 3 * a + b
-                kernels = jnp.concatenate(
-                    [w[e, tap * CH : (tap + 1) * CH, :] for e in chosen], axis=1
-                )
-                r = lax.dot_general(
-                    d, kernels, (((1,), (1,)), ((), ())), preferred_element_type=F32
-                )
-                spread[b, rt * 16 + a : rt * 16 + a + 16, cols, :] += r.reshape(16, 16, CH)
-
-    def x_copies(t, target):
-        _, groups, start = CHUNKS[t // 2]
-        rows = slice(start, start + groups * 16)
-        if t % 2:
-            rows = slice(start + groups * 16, start + groups * 32 + 16)
-        return [
-            along_y(
-                xs.at[mod(gy + d, GY), rows], xr.at[target(d), rows], d,
-                x_s.at[t, d], x_r.at[t, d],
-            )
-            for d in range(1, GY)
-        ]
-
     place16 = lax.broadcasted_iota(jnp.int32, (16, CH), 0)
-    for t in range(TILES):
-        backward(t)
-        first, groups, start = CHUNKS[t // 2]
-        base = start + (t % 2) * groups * 16
-
-        def opened(r):
-            if t % 2 == 0:
-                middle = jnp.where(place16 >= 1, pltpu.roll(spread[1, r, 0:16, :], 1, 0), 0.0)
-                ahead = jnp.where(place16 >= 2, pltpu.roll(spread[2, r, 0:16, :], 2, 0), 0.0)
-                return spread[0, r, 0:16, :] + middle + ahead
-            middle = pltpu.roll(spread[1, r, 8:32, :], 1, 0)[8:24]
-            ahead = pltpu.roll(spread[2, r, 8:32, :], 2, 0)[8:24]
-            return spread[0, r, 16:32, :] + middle + ahead
+
+    def x_rows(rt, half):
+        _, groups, start = CHUNKS[rt]
+        at = start + groups * 16
+        return slice(at, start + groups * 32 + 16) if half else slice(start, at)
+
+    def opened(r, half):
+        if half == 0:
+            middle = jnp.where(place16 >= 1, pltpu.roll(spread[1, r, 0:16, :], 1, 0), 0.0)
+            ahead = jnp.where(place16 >= 2, pltpu.roll(spread[2, r, 0:16, :], 2, 0), 0.0)
+            return spread[0, r, 0:16, :] + middle + ahead
+        middle = pltpu.roll(spread[1, r, 8:32, :], 1, 0)[8:24]
+        ahead = pltpu.roll(spread[2, r, 8:32, :], 2, 0)[8:24]
+        return spread[0, r, 16:32, :] + middle + ahead
+
+    def leave(rt, half):
+        first, groups, start = CHUNKS[rt]
+        base = start + half * groups * 16
 
         def split_group(k, _):
-            lines = [opened(4 * (first + k) + q) for q in range(4)]
+            lines = [opened(4 * (first + k) + q, half) for q in range(4)]
             for jt in range(2):
                 lanes = slice(jt * 128, jt * 128 + 128)
                 for s, part in enumerate(transpose_blocks([line[:, lanes] for line in lines])):
@@ -286,7 +270,7 @@
             return 0
 
         lax.fori_loop(0, groups, split_group, 0, unroll=groups)
-        if t % 2:
+        if half:
             rows = slice(4 * first, 4 * first + 4 * groups)
             last = start + groups * 32
             for jt in range(2):
@@ -302,8 +286,41 @@
                         ]
                 for s, part in enumerate(transpose_blocks([edges[q, jt] for q in range(4)])):
                     xs[jt * 4 + s, last : last + 16, :] = part.astype(BF)
-        for copy in x_copies(t, lambda d: gy):
-            copy.start()
+        rows = x_rows(rt, half)
+        for d in range(1, GY):
+            along_y(
+                xs.at[mod(gy + d, GY), rows], xr.at[gy, rows], d,
+                x_s.at[2 * rt + half], x_r.at[2 * rt + half],
+            ).start()
+
+    for rt in range(3):
+
+        def backward(ct, _):
+            cols = pl.ds(pl.multiple_of(ct * 16, 16), 16)
+            d = jnp.concatenate([deltas[2 * rt + ct, s] for s in range(SLOTS)], axis=1)
+            chosen = [0, 1] + [routes[rt, ct, s - 2] + 2 for s in range(2, SLOTS)]
+            for a in range(3):
+                for b in range(3):
+                    tap = 3 * a + b
+                    kernels = jnp.concatenate(
+                        [w[e, tap * CH : (tap + 1) * CH, :] for e in chosen], axis=1
+                    )
+                    r = lax.dot_general(
+                        d, kernels, (((1,), (1,)), ((), ())), preferred_element_type=F32
+                    )
+                    spread[b, rt * 16 + a : rt * 16 + a + 16, cols, :] += r.reshape(16, 16, CH)
+
+            @pl.when(ct == 0)
+            def _():
+                leave(rt, 0)
+
+            @pl.when(ct == 1)
+            def _():
+                leave(rt, 1)
+
+            return 0
+
+        lax.fori_loop(0, 2, backward, 0)
 
     def own_row(r, _):
         ahead = jnp.where(place > 0, pltpu.roll(spread[2, r], 1, 0), 0.0)
@@ -312,21 +329,20 @@
         return 0
 
     lax.fori_loop(0, ROWS + 2, own_row, 0, unroll=5)
-    erow[0] = total[ROWS + 1].astype(BF)
-    erow[1] = total[0].astype(BF)
+    border_out[0:32] = total[ROWS + 1].astype(BF)
+    border_out[32:64] = total[0].astype(BF)
     for jt in range(2):
         lanes = slice(jt * 128, jt * 128 + 128)
         left_edge[jt, 0 : ROWS + 2] = spread[0, 0 : ROWS + 2, 0, lanes]
-        ecol[0, :, lanes] = edge[1, jt, 1 : ROWS + 1].astype(BF)
-        ecol[1, :, lanes] = left_edge[jt, 1 : ROWS + 1].astype(BF)
+        border_out[64:112, lanes] = edge[1, jt, 1 : ROWS + 1].astype(BF)
+        border_out[112:160, lanes] = left_edge[jt, 1 : ROWS + 1].astype(BF)
         for k, r in enumerate((ROWS + 1, ROWS + 1, 0, 0)):
             corner = left_edge[jt, r : r + 1, :] if k % 2 else edge[1, jt, r : r + 1, :]
-            ecor[k, :, lanes] = jnp.broadcast_to(corner, (16, 128)).astype(BF)
-    border = border_copies(
-        gx, gy,
-        [erow.at[0], erow.at[1], ecol.at[0], ecol.at[1]] + [ecor.at[k] for k in range(4)],
-        [brow.at[0], brow.at[1], bcol.at[0], bcol.at[1]] + [bcor.at[k] for k in range(4)],
-        border_s, border_r,
+            border_out[160 + 16 * k : 176 + 16 * k, lanes] = jnp.broadcast_to(
+                corner, (16, 128)
+            ).astype(BF)
+    border, border_all = border_copies(
+        gx, gy, border_out, border_in, border_s.at[0], border_r.at[0]
     )
     for copy in border:
         copy.start()
@@ -335,10 +351,10 @@
     for copy in in_copies[2:]:
         copy.wait()
     for chunk, (first, groups, start) in enumerate(CHUNKS):
-        for copy in x_copies(2 * chunk, lambda d: mod(gy - d, GY)):
-            copy.wait()
-        for copy in x_copies(2 * chunk + 1, lambda d: mod(gy - d, GY)):
-            copy.wait()
+        for part in range(2):
+            rows = x_rows(chunk, part)
+            t = 2 * chunk + part
+            along_y(xs.at[1:GY, rows], xr.at[1:GY, rows], 1, x_s.at[t], x_r.at[t]).wait()
         last = start + groups * 32
         rim = jnp.dot(
             edge_table[0 : groups * 64],
@@ -373,36 +389,34 @@
                 cs[mh * 8 + 2 * pair + k] = c[mh * 64 : mh * 64 + 64, k * 128 : k * 128 + 128]
     parts_of = [slice(0, 32), slice(32, 64)]
 
-    def c_copy(part, d, target):
+    def c_copy(part, source, target, d=1):
         rows = parts_of[part]
-        return along_x(
-            cs.at[mod(gx + d, GX), rows], cr.at[target, rows], d, c_s.at[part, d], c_r.at[part, d]
-        )
-
-    def g_copy(part, d, target):
+        return along_x(cs.at[source, rows], cr.at[target, rows], d, c_s.at[part], c_r.at[part])
+
+    def g_copy(part, source, target, d=1):
         rows = parts_of[part]
-        return along_y(cg.at[gy, rows], cg.at[target, rows], d, g_s.at[part, d], g_r.at[part, d])
-
-    def p_copy(part, d, target):
+        return along_y(cg.at[source, rows], cg.at[target, rows], d, g_s.at[part], g_r.at[part])
+
+    def p_copy(part, source, target, d=1):
         rows = parts_of[part]
-        return along_x(sp.at[gx, rows], sp.at[target, rows], d, p_s.at[part, d], p_r.at[part, d])
-
+        return along_x(sp.at[source, rows], sp.at[target, rows], d, p_s.at[part], p_r.at[part])
+
+    others_x, others_y = slice(1, GX), slice(1, GY)
     for part in range(2):
         for d in range(1, GX):
-            c_copy(part, d, gx).start()
+            c_copy(part, mod(gx + d, GX), gx, d).start()
     cr[gx] = cs[gx]
 
-    for copy in border:
-        copy.wait()
-    total[1] += brow[0].astype(F32) * above
-    total[ROWS] += brow[1].astype(F32) * below
+    border_all.wait()
+    total[1] += border_in[0:32].astype(F32) * above
+    total[ROWS] += border_in[32:64].astype(F32) * below
     own = slice(1, ROWS + 1)
-    total[own, 0, :] += bcol[0].astype(F32) * left
-    total[own, COLS - 1, :] += bcol[1].astype(F32) * right
-    total[1, 0:1, :] += bcor[0][0:1].astype(F32) * (above * left)
-    total[1, COLS - 1 : COLS, :] += bcor[1][0:1].astype(F32) * (above * right)
-    total[ROWS, 0:1, :] += bcor[2][0:1].astype(F32) * (below * left)
-    total[ROWS, COLS - 1 : COLS, :] += bcor[3][0:1].astype(F32) * (below * right)
+    total[own, 0, :] += border_in[64:112].astype(F32) * left
+    total[own, COLS - 1, :] += border_in[112:160].astype(F32) * right
+    total[1, 0:1, :] += border_in[160:176].astype(F32)[0:1] * (above * left)
+    total[1, COLS - 1 : COLS, :] += border_in[176:192].astype(F32)[0:1] * (above * right)
+    total[ROWS, 0:1, :] += border_in[192:208].astype(F32)[0:1] * (below * left)
+    total[ROWS, COLS - 1 : COLS, :] += border_in[208:224].astype(F32)[0:1] * (below * right)
 
     n8 = lax.rem(gx, 8)
     mh = gx // 8
@@ -417,20 +431,18 @@
 
     for part in range(2):
         rows = parts_of[part]
-        for d in range(1, GX):
-            c_copy(part, d, mod(gx - d, GX)).wait()
+        c_copy(part, others_x, others_x).wait()
         coef = cr[0, rows].astype(F32)
         for k in range(1, GX):
             coef = coef + cr[k, rows].astype(F32)
         cg[gy, rows] = coef.astype(BF)
         for d in range(1, GY):
-            g_copy(part, d, gy).start()
+            g_copy(part, gy, gy, d).start()
 
     mixer = band[...].reshape(512, CH)
     for part in range(2):
         rows = parts_of[part]
-        for d in range(1, GY):
-            g_copy(part, d, mod(gy - d, GY)).wait()
+        g_copy(part, others_y, others_y).wait()
         inputs = [
             transpose_blocks([cg[jt * 4 + p, rows].astype(F32) for p in range(4)])
             for jt in range(2)
@@ -451,10 +463,9 @@
             spec = jnp.where(lane_block == n4, y, spec)
         sp[gx, rows] = spec.astype(BF)
         for d in range(1, GX):
-            p_copy(part, d, gx).start()
+            p_copy(part, gx, gx, d).start()
     for part in range(2):
-        for d in range(1, GX):
-            p_copy(part, d, mod(gx - d, GX)).wait()
+        p_copy(part, others_x, others_x).wait()
 
     inverse_scale = 1.0 / math.sqrt(2 * KH * KW)
     for pair in range(4):
@@ -466,15 +477,9 @@
         for k in range(2):
             zs[(2 * pair + k) * 96 : (2 * pair + k + 1) * 96, :] = z[:, k * 128 : k * 128 + 128]
 
-    def f_copies(third, target):
+    def f_copy(third, source, target, d=1):
         rows = slice(4 * third, 4 * third + 4)
-        return [
-            along_y(
-                fs.at[mod(gy + d, GY), rows], fr.at[target(d), rows], d,
-                f_s.at[third, d], f_r.at[third, d],
-            )
-            for d in range(1, GY)
-        ]
+        return along_y(fs.at[source, rows], fr.at[target, rows], d, f_s.at[third], f_r.at[third])
 
     for third in range(3):
         for pair in range(2 * third, 2 * third + 2):
@@ -491,8 +496,8 @@
             for k in range(2):
                 for j in range(GY):
                     fs[j, 2 * pair + k] = f[j * 32 : j * 32 + 32, k * 128 : k * 128 + 128]
-        for copy in f_copies(third, lambda d: gy):
-            copy.start()
+        for d in range(1, GY):
+            f_copy(third, mod(gy + d, GY), gy, d).start()
     fr[gy] = fs[gy]
 
     def join_group(g, _):
@@ -504,8 +509,7 @@
         return 0
 
     for third in range(3):
-        for copy in f_copies(third, lambda d: mod(gy - d, GY)):
-            copy.wait()
+        f_copy(third, others_y, others_y).wait()
         lax.fori_loop(4 * third, 4 * third + 4, join_group, 0, unroll=2)
 
 
@@ -516,15 +520,6 @@
 
 def dma(*shape):
     return pltpu.SemaphoreType.DMA(shape)
-
-
-def border(count=1):
-    one = [
-        pltpu.VMEM((2, COLS, CH), BF),
-        pltpu.VMEM((2, ROWS, CH), BF),
-        pltpu.VMEM((4, 16, CH), BF),
-    ]
-    return one * count
 
 
 def body(saved_mid, out_grad, expert_weight, routes, gates, band_matrix, band_ids):
@@ -553,7 +548,7 @@
             pltpu.VMEM((2, 2, OPEN + 4, 128), F32),
             pltpu.VMEM((4, 2, 16, 128), F32),
             pltpu.VMEM((2, OPEN + 4, 128), F32),
-            *border(4),
+            *[pltpu.VMEM((224, CH), BF)] * 4,
             pltpu.VMEM((GY, 464, 128), BF),
             pltpu.VMEM((GY, 464, 128), BF),
             pltpu.VMEM((8 * 2 * OPEN, 128), F32),
@@ -564,9 +559,8 @@
             pltpu.VMEM((8 * 2 * ROWS, 128), F32),
             pltpu.VMEM((GY, 12, 32, 128), BF),
             pltpu.VMEM((GY, 12, 32, 128), BF),
-            dma(EXPERTS), dma(8), dma(8), dma(8), dma(8), dma(8),
-            dma(6, GY), dma(6, GY), dma(2, GX), dma(2, GX), dma(2, GY), dma(2, GY),
-            dma(2, GX), dma(2, GX), dma(3, GY), dma(3, GY),
+            dma(3), dma(8), dma(1), dma(1), dma(1), dma(1),
+            dma(6), dma(6), dma(2), dma(2), dma(2), dma(2), dma(2), dma(2), dma(3), dma(3),
         ],
         compiler_params=pltpu.CompilerParams(
             collective_id=0, has_side_effects=True, vmem_limit_bytes=66_000_000

time: 89 us -> 76.1 us (0.86)
  Pallas kernels: 87.9 us -> 75.1 us
    pallas_call x1, Pallas kernels: 87.9 us -> 75.1 us  [body(): pl.pallas_call(fused_body, name='fused', out_shape=pltpu.VMEM((ROWS, COLS...]
where the time goes in v4:
time: 76.1 us; the launch traced here: 75.9 us
  Pallas kernels  75.1 us (99%)
  local copies, waits for them, and re-layouts  0.88 us (1%)
    pallas_call x1, Pallas kernels, body(): pl.pallas_call(fused_body, name='fused', out_shape=pltpu.VMEM((ROWS, COLS...  75.1 us

profile of v4, /device:TPU:0, one launch (start us, length us, event | category | flops | bytes accessed | tf_op | source)
XLA Modules:
  0.0 75.9 jit_solution(6880376336545169955)
XLA Ops:
  0.0 75.1 %fused.1 = bf16[48,32,256]{2,1,0:T(8,128)(2,1)S(1)} custom-call(bf16[48,32,256]{2,1,0:T(8,128)(2,1)} %mid_hbm.1, bf16[48,32,256]{2,1,0:T(8,128)(2,1)} %grad_hbm.1, bf16[10,2304,256]{2,1,0:T(8,128)(2,1)} %bitcast.2, s32[3,2,4]{2,1,0:T(2,128)} %routes.1, f32[3,2,6]{2,1,0:T(2,128)} %gates.1, bf16[16,256,256]{2,1,0:T(8,128)(2,1)} %band_hbm.1, s32[32,64]{1,0:T(8,128)} %bitcast.3, ...), custom_call_target="tpu_custom_call" | custom-call | tf_op jit(solution)/shard_map/fused/pallas_call | solution.py:526
  75.1 0.9 %copy.14 = bf16[48,32,256]{2,1,0:T(8,128)(2,1)} copy(bf16[48,32,256]{2,1,0:T(8,128)(2,1)S(1)} %fused.1) | data formatting | bytes 1572864

commit v5 on v4

--- a/solution.py
+++ b/solution.py
@@ -20,6 +20,8 @@
 CHUNKS = ((0, 4, 0), (4, 4, 144), (8, 5, 288))
 
 DIRS = ((1, 0), (-1, 0), (0, 1), (0, -1), (1, 1), (1, -1), (-1, 1), (-1, -1))
+AHEAD_X = (8, 10, 6, 9, 7, 11, 5, 12, 4, 13, 3, 14, 2, 15, 1)
+AHEAD_Y = (4, 5, 3, 6, 2, 7, 1)
 PARTS = ((0, 32), (32, 64), (64, 112), (112, 160), (160, 176), (176, 192), (192, 208), (208, 224))
 
 
@@ -117,10 +119,10 @@
 
 
 def fused_body(
-    mid_hbm, grad_hbm, w_hbm, routes, gates, band_hbm, band_ids,
+    mid_hbm, grad_hbm, w_hbm, routes_hbm, gates_hbm, band_hbm, ids_hbm,
     col_hbm, col_t_hbm, edge_hbm, row_hbm, back_hbm,
     out,
-    mid, grad, w, row, back, band, col, col_t, edge_table, ext, shifted, side, deltas, spread, total, edge, edges, left_edge,
+    routes, gates, band_ids, mid, grad, w, row, back, band, col, col_t, edge_table, shifted, side, deltas, last_pre, spread, total, edge, edges, left_edge,
     border_out, border_in, halo_out, halo_in,
     xs, xr, half, cs, cr, cg, sp, zs, fs, fr,
     w_sem, in_sem, halo_s, halo_r, border_s, border_r,
@@ -134,14 +136,14 @@
     sources = [
         mid_hbm, grad_hbm, row_hbm.at[gx], back_hbm.at[gx],
         band_hbm.at[:, pl.ds(pl.multiple_of(gy * 32, 32), 32), :],
-        col_hbm, col_t_hbm, edge_hbm,
+        col_hbm, col_t_hbm, edge_hbm, ids_hbm, routes_hbm, gates_hbm,
     ]
-    targets = [mid, grad, row, back, band, col, col_t, edge_table]
+    targets = [mid, grad, row, back, band, col, col_t, edge_table, band_ids, routes, gates]
     in_copies = [
         pltpu.make_async_copy(source, target, in_sem.at[k])
         for k, (source, target) in enumerate(zip(sources, targets))
     ]
-    for copy in in_copies[:1] + w_copies[:1] + in_copies[1:2] + w_copies[1:] + in_copies[2:]:
+    for copy in in_copies[:1] + w_copies[:1] + in_copies[9:] + in_copies[1:2] + w_copies[1:] + in_copies[2:9]:
         copy.start()
     barrier = pltpu.get_barrier_semaphore()
     partners = [(gx, mod(gy + d, GY)) for d in range(1, GY)]
@@ -156,13 +158,13 @@
     right = jnp.where(gy < GY - 1, 1.0, 0.0)
 
     in_copies[0].wait()
-    ext[1 : ROWS + 1] = mid[...].astype(F32)
     halo_out[0:32] = mid[ROWS - 1]
     halo_out[32:64] = mid[0]
-    halo_out[64:112] = ext[1 : ROWS + 1, COLS - 1, :].astype(BF)
-    halo_out[112:160] = ext[1 : ROWS + 1, 0, :].astype(BF)
-    for k, (r, c) in enumerate(((ROWS, COLS - 1), (ROWS, 0), (1, COLS - 1), (1, 0))):
-        corner = jnp.broadcast_to(ext[r, c : c + 1, :], (16, CH)).astype(BF)
+    rim = [mid[:, 16:32, :].astype(F32)[:, 15, :], mid[:, 0:16, :].astype(F32)[:, 0, :]]
+    halo_out[64:112] = rim[0].astype(BF)
+    halo_out[112:160] = rim[1].astype(BF)
+    for k, r in enumerate((ROWS - 1, ROWS - 1, 0, 0)):
+        corner = jnp.broadcast_to(rim[k % 2][r : r + 1], (16, CH)).astype(BF)
         halo_out[160 + 16 * k : 176 + 16 * k] = corner
     pl.semaphore_wait(barrier, len(partners))
     halo, halo_all = border_copies(gx, gy, halo_out, halo_in, halo_s.at[0], halo_r.at[0])
@@ -175,30 +177,49 @@
     spread[1, 1 : ROWS + 1] = grad[...].astype(F32)
     spread[1, ROWS + 1 :] = jnp.zeros((OPEN - ROWS - 1, COLS, CH), F32)
     edges[...] = jnp.zeros_like(edges)
+    last_pre[...] = jnp.zeros_like(last_pre)
+    place = lax.broadcasted_iota(jnp.int32, (COLS, CH), 0)
+
+    def shift_row(r, line):
+        shifted[1, r] = line.astype(BF)
+        shifted[0, r] = pltpu.roll(line, 1, 0).astype(BF)
+        shifted[2, r] = pltpu.roll(line, COLS - 1, 0).astype(BF)
+
+    def own_shift(r, _):
+        shift_row(r + 1, mid[r].astype(F32))
+        return 0
+
+    lax.fori_loop(0, ROWS, own_shift, 0, unroll=4)
     halo_all.wait()
-    ext[0] = halo_in[0:32].astype(F32) * above
-    ext[ROWS + 1] = halo_in[32:64].astype(F32) * below
+    shift_row(0, halo_in[0:32].astype(F32) * above)
+    shift_row(ROWS + 1, halo_in[32:64].astype(F32) * below)
     side[0, 8 : 8 + ROWS] = halo_in[64:112].astype(F32) * left
     side[1, 8 : 8 + ROWS] = halo_in[112:160].astype(F32) * right
     side[0, 7:8] = halo_in[160:176].astype(F32)[0:1] * (above * left)
     side[1, 7:8] = halo_in[176:192].astype(F32)[0:1] * (above * right)
     side[0, 8 + ROWS : 9 + ROWS] = halo_in[192:208].astype(F32)[0:1] * (below * left)
     side[1, 8 + ROWS : 9 + ROWS] = halo_in[208:224].astype(F32)[0:1] * (below * right)
-    place = lax.broadcasted_iota(jnp.int32, (COLS, CH), 0)
-
-    def shift_row(r, _):
-        line = ext[r]
+    place16 = lax.broadcasted_iota(jnp.int32, (16, CH), 0)
+
+    def fix_row(r, _):
         before = side[0, pl.ds(r + 7, 1), :]
         after = side[1, pl.ds(r + 7, 1), :]
-        shifted[1, r] = line.astype(BF)
-        shifted[0, r] = jnp.where(place == 0, before, pltpu.roll(line, 1, 0)).astype(BF)
-        shifted[2, r] = jnp.where(place == COLS - 1, after, pltpu.roll(line, COLS - 1, 0)).astype(BF)
+        first = shifted[0, r, 0:16, :].astype(F32)
+        shifted[0, r, 0:16, :] = jnp.where(place16 == 0, before, first).astype(BF)
+        last = shifted[2, r, 16:32, :].astype(F32)
+        shifted[2, r, 16:32, :] = jnp.where(place16 == 15, after, last).astype(BF)
         return 0
 
-    lax.fori_loop(0, ROWS + 2, shift_row, 0, unroll=5)
+    lax.fori_loop(0, ROWS + 2, fix_row, 0, unroll=5)
 
     def expert(t, s):
         return routes[t // 2, t % 2, s - 2] + 2
+
+    def slope(t, s, pre):
+        rt, cols = t // 2, slice((t % 2) * 16, (t % 2) * 16 + 16)
+        g = grad[rt * 16 : rt * 16 + 16, cols, :].reshape(256, CH).astype(F32)
+        gate = gates[rt, t % 2, s] * 0.5
+        deltas[t, s] = (gelu_slope_twice(pre) * (g * gate)).astype(BF)
 
     def forward(s, kernel_of):
         for t in range(TILES):
@@ -211,9 +232,12 @@
             pre = jnp.dot(
                 jnp.concatenate(pieces, axis=1), w[kernel_of(t, s)], preferred_element_type=F32
             )
-            g = grad[rt * 16 : rt * 16 + 16, cols, :].reshape(256, CH).astype(F32)
-            gate = gates[rt, t % 2, s] * 0.5
-            deltas[t, s] = (gelu_slope_twice(pre) * (g * gate)).astype(BF)
+            if t == 0:
+                slope(TILES - 1, jnp.maximum(s - 1, 0), last_pre[...])
+            if t < TILES - 1:
+                slope(t, s, pre)
+            else:
+                last_pre[...] = pre
 
     def forward_shared(s, _):
         forward(s, lambda t, s: s)
@@ -225,9 +249,12 @@
 
     w_copies[0].wait()
     w_copies[1].wait()
+    in_copies[9].wait()
+    in_copies[10].wait()
     lax.fori_loop(0, 2, forward_shared, 0)
     w_copies[2].wait()
     lax.fori_loop(2, SLOTS, forward_routed, 0)
+    slope(TILES - 1, SLOTS - 1, last_pre[...])
 
     def along_y(source, target, d, send, recv):
         return pltpu.make_async_remote_copy(
@@ -240,8 +267,6 @@
             src_ref=source, dst_ref=target, send_sem=send, recv_sem=recv,
             device_id=(mod(gx + d, GX), gy), device_id_type=MESH,
         )
-
-    place16 = lax.broadcasted_iota(jnp.int32, (16, CH), 0)
 
     def x_rows(rt, half):
         _, groups, start = CHUNKS[rt]
@@ -287,7 +312,7 @@
                 for s, part in enumerate(transpose_blocks([edges[q, jt] for q in range(4)])):
                     xs[jt * 4 + s, last : last + 16, :] = part.astype(BF)
         rows = x_rows(rt, half)
-        for d in range(1, GY):
+        for d in AHEAD_Y:
             along_y(
                 xs.at[mod(gy + d, GY), rows], xr.at[gy, rows], d,
                 x_s.at[2 * rt + half], x_r.at[2 * rt + half],
@@ -348,7 +373,7 @@
         copy.start()
     xr[gy] = xs[gy]
 
-    for copy in in_copies[2:]:
+    for copy in in_copies[2:9]:
         copy.wait()
     for chunk, (first, groups, start) in enumerate(CHUNKS):
         for part in range(2):
@@ -403,7 +428,7 @@
 
     others_x, others_y = slice(1, GX), slice(1, GY)
     for part in range(2):
-        for d in range(1, GX):
+        for d in AHEAD_X:
             c_copy(part, mod(gx + d, GX), gx, d).start()
     cr[gx] = cs[gx]
 
@@ -436,7 +461,7 @@
         for k in range(1, GX):
             coef = coef + cr[k, rows].astype(F32)
         cg[gy, rows] = coef.astype(BF)
-        for d in range(1, GY):
+        for d in AHEAD_Y:
             g_copy(part, gy, gy, d).start()
 
     mixer = band[...].reshape(512, CH)
@@ -462,7 +487,7 @@
             y = y + pltpu.roll(y, 32, 1)
             spec = jnp.where(lane_block == n4, y, spec)
         sp[gx, rows] = spec.astype(BF)
-        for d in range(1, GX):
+        for d in AHEAD_X:
             p_copy(part, gx, gx, d).start()
     for part in range(2):
         p_copy(part, others_x, others_x).wait()
@@ -477,12 +502,12 @@
         for k in range(2):
             zs[(2 * pair + k) * 96 : (2 * pair + k + 1) * 96, :] = z[:, k * 128 : k * 128 + 128]
 
-    def f_copy(third, source, target, d=1):
-        rows = slice(4 * third, 4 * third + 4)
-        return along_y(fs.at[source, rows], fr.at[target, rows], d, f_s.at[third], f_r.at[third])
-
-    for third in range(3):
-        for pair in range(2 * third, 2 * third + 2):
+    def f_copy(sixth, source, target, d=1):
+        rows = slice(2 * sixth, 2 * sixth + 2)
+        return along_y(fs.at[source, rows], fr.at[target, rows], d, f_s.at[sixth], f_r.at[sixth])
+
+    for sixth in range(6):
+        for pair in (sixth,):
             columns = []
             for k in range(2):
                 pieces = []
@@ -496,8 +521,8 @@
             for k in range(2):
                 for j in range(GY):
                     fs[j, 2 * pair + k] = f[j * 32 : j * 32 + 32, k * 128 : k * 128 + 128]
-        for d in range(1, GY):
-            f_copy(third, mod(gy + d, GY), gy, d).start()
+        for d in AHEAD_Y:
+            f_copy(sixth, mod(gy + d, GY), gy, d).start()
     fr[gy] = fs[gy]
 
     def join_group(g, _):
@@ -508,13 +533,11 @@
                 out[4 * g + q, :, lanes] = (total[4 * g + q + 1, :, lanes] + part).astype(BF)
         return 0
 
-    for third in range(3):
-        f_copy(third, others_y, others_y).wait()
-        lax.fori_loop(4 * third, 4 * third + 4, join_group, 0, unroll=2)
-
-
-VMEM = pl.BlockSpec(memory_space=pltpu.VMEM)
-SMEM = pl.BlockSpec(memory_space=pltpu.SMEM)
+    for sixth in range(6):
+        f_copy(sixth, others_y, others_y).wait()
+        lax.fori_loop(2 * sixth, 2 * sixth + 2, join_group, 0, unroll=2)
+
+
 ANY = pl.BlockSpec(memory_space=pl.ANY)
 
 
@@ -527,9 +550,12 @@
         fused_body,
         name="fused",
         out_shape=pltpu.VMEM((ROWS, COLS, CH), BF),
-        in_specs=[ANY, ANY, ANY, SMEM, SMEM, ANY, VMEM, ANY, ANY, ANY, ANY, ANY],
-        out_specs=VMEM,
+        in_specs=[ANY, ANY, ANY, ANY, ANY, ANY, ANY, ANY, ANY, ANY, ANY, ANY],
+        out_specs=pl.BlockSpec(memory_space=pltpu.VMEM),
         scratch_shapes=[
+            pltpu.SMEM((3, 2, 4), jnp.int32),
+            pltpu.SMEM((3, 2, SLOTS), F32),
+            pltpu.VMEM((KW, KH), jnp.int32),
             pltpu.VMEM((ROWS, COLS, CH), BF),
             pltpu.VMEM((ROWS, COLS, CH), BF),
             pltpu.VMEM((EXPERTS, 9 * CH, CH), BF),
@@ -539,10 +565,10 @@
             pltpu.VMEM((64, 256), BF),
             pltpu.VMEM((256, 64), BF),
             pltpu.VMEM((320, 128), BF),
-            pltpu.VMEM((ROWS + 2, COLS, CH), F32),
             pltpu.VMEM((3, ROWS + 2, COLS, CH), BF),
             pltpu.VMEM((2, 64, CH), F32),
             pltpu.VMEM((TILES, SLOTS, 256, CH), BF),
+            pltpu.VMEM((256, CH), F32),
             pltpu.VMEM((3, OPEN, COLS, CH), F32),
             pltpu.VMEM((OPEN, COLS, CH), F32),
             pltpu.VMEM((2, 2, OPEN + 4, 128), F32),
@@ -559,8 +585,8 @@
             pltpu.VMEM((8 * 2 * ROWS, 128), F32),
             pltpu.VMEM((GY, 12, 32, 128), BF),
             pltpu.VMEM((GY, 12, 32, 128), BF),
-            dma(3), dma(8), dma(1), dma(1), dma(1), dma(1),
-            dma(6), dma(6), dma(2), dma(2), dma(2), dma(2), dma(2), dma(2), dma(3), dma(3),
+            dma(3), dma(11), dma(1), dma(1), dma(1), dma(1),
+            dma(6), dma(6), dma(2), dma(2), dma(2), dma(2), dma(2), dma(2), dma(6), dma(6),
         ],
         compiler_params=pltpu.CompilerParams(
             collective_id=0, has_side_effects=True, vmem_limit_bytes=66_000_000

time: 76.1 us -> 74.2 us (0.975)
  Pallas kernels: 75.1 us -> 73 us
    pallas_call x1, Pallas kernels: 75.1 us -> 73 us  [body(): pl.pallas_call(fused_body, name='fused', out_shape=pltpu.VMEM((ROWS, COLS...]
where the time goes in v5:
time: 74.2 us; the launch traced here: 73.9 us
  Pallas kernels  73 us (98%)
  local copies, waits for them, and re-layouts  0.88 us (1%)
    pallas_call x1, Pallas kernels, body(): pl.pallas_call(fused_body, name='fused', out_shape=pltpu.VMEM((ROWS, COLS...  73 us

profile of v5, /device:TPU:0, one launch (start us, length us, event | category | flops | bytes accessed | tf_op | source)
XLA Modules:
  0.0 73.9 jit_solution(15893284567664125086)
XLA Ops:
  0.0 73.0 %fused.1 = bf16[48,32,256]{2,1,0:T(8,128)(2,1)S(1)} custom-call(bf16[48,32,256]{2,1,0:T(8,128)(2,1)} %mid_hbm.1, bf16[48,32,256]{2,1,0:T(8,128)(2,1)} %grad_hbm.1, bf16[10,2304,256]{2,1,0:T(8,128)(2,1)} %bitcast.2, s32[3,2,4]{2,1,0:T(2,128)} %routes_hbm.1, f32[3,2,6]{2,1,0:T(2,128)} %gates_hbm.1, bf16[16,256,256]{2,1,0:T(8,128)(2,1)} %band_hbm.1, ...), custom_call_target="tpu_custom_call" | custom-call | tf_op jit(solution)/shard_map/fused/pallas_call | solution.py:549
  73.1 0.9 %copy.14 = bf16[48,32,256]{2,1,0:T(8,128)(2,1)} copy(bf16[48,32,256]{2,1,0:T(8,128)(2,1)S(1)} %fused.1) | data formatting | bytes 1572864

commit v6 on v5

--- a/solution.py
+++ b/solution.py
@@ -17,6 +17,7 @@
 H, W = 768, 256
 EXPERTS, SLOTS, TILES = 10, 6, 6
 OPEN = ROWS + 4
+PIECES = 4
 CHUNKS = ((0, 4, 0), (4, 4, 144), (8, 5, 288))
 
 DIRS = ((1, 0), (-1, 0), (0, 1), (0, -1), (1, 1), (1, -1), (-1, 1), (-1, -1))
@@ -143,14 +144,15 @@
         pltpu.make_async_copy(source, target, in_sem.at[k])
         for k, (source, target) in enumerate(zip(sources, targets))
     ]
-    for copy in in_copies[:1] + w_copies[:1] + in_copies[9:] + in_copies[1:2] + w_copies[1:] + in_copies[2:9]:
-        copy.start()
+    in_copies[0].start()
     barrier = pltpu.get_barrier_semaphore()
-    partners = [(gx, mod(gy + d, GY)) for d in range(1, GY)]
-    partners += [(mod(gx + d, GX), gy) for d in range(1, GX)]
-    partners += [(mod(gx + dr, GX), mod(gy + dc, GY)) for dr, dc in DIRS[4:]]
+    partners = [(mod(gx + dr, GX), mod(gy + dc, GY)) for dr, dc in DIRS]
+    partners += [(mod(gx + d, GX), gy) for d in range(2, GX - 1)]
+    partners += [(gx, mod(gy + d, GY)) for d in range(2, GY - 1)]
     for device in partners:
         pl.semaphore_signal(barrier, inc=1, device_id=device, device_id_type=MESH)
+    for copy in w_copies[:1] + in_copies[9:] + in_copies[1:2] + w_copies[1:] + in_copies[2:9]:
+        copy.start()
 
     above = jnp.where(gx > 0, 1.0, 0.0)
     below = jnp.where(gx < GX - 1, 1.0, 0.0)
@@ -215,29 +217,33 @@
     def expert(t, s):
         return routes[t // 2, t % 2, s - 2] + 2
 
-    def slope(t, s, pre):
-        rt, cols = t // 2, slice((t % 2) * 16, (t % 2) * 16 + 16)
-        g = grad[rt * 16 : rt * 16 + 16, cols, :].reshape(256, CH).astype(F32)
-        gate = gates[rt, t % 2, s] * 0.5
-        deltas[t, s] = (gelu_slope_twice(pre) * (g * gate)).astype(BF)
+    def slope(t, s, pre, low=0, high=16):
+        top = (t // 2) * 16
+        cols = slice((t % 2) * 16, (t % 2) * 16 + 16)
+        g = grad[top + low : top + high, cols, :].reshape(-1, CH).astype(F32)
+        gate = gates[t // 2, t % 2, s] * 0.5
+        values = (gelu_slope_twice(pre) * (g * gate)).astype(BF)
+        deltas[t, s, low * 16 : high * 16] = values
 
     def forward(s, kernel_of):
         for t in range(TILES):
-            rt, cols = t // 2, slice((t % 2) * 16, (t % 2) * 16 + 16)
-            pieces = [
-                shifted[b, rt * 16 + a : rt * 16 + a + 16, cols, :].reshape(256, CH)
-                for a in range(3)
-                for b in range(3)
-            ]
-            pre = jnp.dot(
-                jnp.concatenate(pieces, axis=1), w[kernel_of(t, s)], preferred_element_type=F32
-            )
-            if t == 0:
-                slope(TILES - 1, jnp.maximum(s - 1, 0), last_pre[...])
-            if t < TILES - 1:
-                slope(t, s, pre)
-            else:
-                last_pre[...] = pre
+            top = (t // 2) * 16
+            cols = slice((t % 2) * 16, (t % 2) * 16 + 16)
+            for low in (0, 8):
+                pieces = [
+                    shifted[b, top + low + a : top + low + a + 8, cols, :].reshape(128, CH)
+                    for a in range(3)
+                    for b in range(3)
+                ]
+                pre = jnp.dot(
+                    jnp.concatenate(pieces, axis=1), w[kernel_of(t, s)], preferred_element_type=F32
+                )
+                if t == 0 and low == 0:
+                    slope(TILES - 1, jnp.maximum(s - 1, 0), last_pre[...], 8)
+                if t < TILES - 1 or low == 0:
+                    slope(t, s, pre, low, low + 8)
+                else:
+                    last_pre[...] = pre
 
     def forward_shared(s, _):
         forward(s, lambda t, s: s)
@@ -254,7 +260,7 @@
     lax.fori_loop(0, 2, forward_shared, 0)
     w_copies[2].wait()
     lax.fori_loop(2, SLOTS, forward_routed, 0)
-    slope(TILES - 1, SLOTS - 1, last_pre[...])
+    slope(TILES - 1, SLOTS - 1, last_pre[...], 8)
 
     def along_y(source, target, d, send, recv):
         return pltpu.make_async_remote_copy(
@@ -412,7 +418,8 @@
         for k in range(2):
             for mh in range(2):
                 cs[mh * 8 + 2 * pair + k] = c[mh * 64 : mh * 64 + 64, k * 128 : k * 128 + 128]
-    parts_of = [slice(0, 32), slice(32, 64)]
+    halves_of = [slice(0, 32), slice(32, 64)]
+    parts_of = [slice(16 * k, 16 * k + 16) for k in range(PIECES)]
 
     def c_copy(part, source, target, d=1):
         rows = parts_of[part]
@@ -423,11 +430,11 @@
         return along_y(cg.at[source, rows], cg.at[target, rows], d, g_s.at[part], g_r.at[part])
 
     def p_copy(part, source, target, d=1):
-        rows = parts_of[part]
+        rows = halves_of[part]
         return along_x(sp.at[source, rows], sp.at[target, rows], d, p_s.at[part], p_r.at[part])
 
     others_x, others_y = slice(1, GX), slice(1, GY)
-    for part in range(2):
+    for part in range(PIECES):
         for d in AHEAD_X:
             c_copy(part, mod(gx + d, GX), gx, d).start()
     cr[gx] = cs[gx]
@@ -454,7 +461,7 @@
         ids = jnp.broadcast_to(band_ids[pl.ds(4 * n8 + n4, 1), :], (32, KH))
         band_of.append(jnp.sum(jnp.where(lane64 == row64 + 32 * mh, ids, 0), axis=1, keepdims=True))
 
-    for part in range(2):
+    for part in range(PIECES):
         rows = parts_of[part]
         c_copy(part, others_x, others_x).wait()
         coef = cr[0, rows].astype(F32)
@@ -466,8 +473,9 @@
 
     mixer = band[...].reshape(512, CH)
     for part in range(2):
-        rows = parts_of[part]
-        g_copy(part, others_y, others_y).wait()
+        rows = halves_of[part]
+        for piece in range(part * PIECES // 2, (part + 1) * PIECES // 2):
+            g_copy(piece, others_y, others_y).wait()
         inputs = [
             transpose_blocks([cg[jt * 4 + p, rows].astype(F32) for p in range(4)])
             for jt in range(2)
@@ -568,7 +576,7 @@
             pltpu.VMEM((3, ROWS + 2, COLS, CH), BF),
             pltpu.VMEM((2, 64, CH), F32),
             pltpu.VMEM((TILES, SLOTS, 256, CH), BF),
-            pltpu.VMEM((256, CH), F32),
+            pltpu.VMEM((128, CH), F32),
             pltpu.VMEM((3, OPEN, COLS, CH), F32),
             pltpu.VMEM((OPEN, COLS, CH), F32),
             pltpu.VMEM((2, 2, OPEN + 4, 128), F32),
@@ -586,7 +594,7 @@
             pltpu.VMEM((GY, 12, 32, 128), BF),
             pltpu.VMEM((GY, 12, 32, 128), BF),
             dma(3), dma(11), dma(1), dma(1), dma(1), dma(1),
-            dma(6), dma(6), dma(2), dma(2), dma(2), dma(2), dma(2), dma(2), dma(6), dma(6),
+            dma(6), dma(6), *[dma(PIECES)] * 4, dma(2), dma(2), dma(6), dma(6),
         ],
         compiler_params=pltpu.CompilerParams(
             collective_id=0, has_side_effects=True, vmem_limit_bytes=66_000_000

time: 74.2 us -> 73.7 us (level)
  no operation moved by 1% of the time
where the time goes in v6:
time: 73.7 us; the launch traced here: 73.5 us
  Pallas kernels  72.6 us (99%)
  local copies, waits for them, and re-layouts  0.88 us (1%)
    pallas_call x1, Pallas kernels, body(): pl.pallas_call(fused_body, name='fused', out_shape=pltpu.VMEM((ROWS, COLS...  72.6 us

profile of v6, /device:TPU:0, one launch (start us, length us, event | category | flops | bytes accessed | tf_op | source)
XLA Modules:
  0.0 73.5 jit_solution(166047241882862005)
XLA Ops:
  0.0 72.6 %fused.1 = bf16[48,32,256]{2,1,0:T(8,128)(2,1)S(1)} custom-call(bf16[48,32,256]{2,1,0:T(8,128)(2,1)} %mid_hbm.1, bf16[48,32,256]{2,1,0:T(8,128)(2,1)} %grad_hbm.1, bf16[10,2304,256]{2,1,0:T(8,128)(2,1)} %bitcast.2, s32[3,2,4]{2,1,0:T(2,128)} %routes_hbm.1, f32[3,2,6]{2,1,0:T(2,128)} %gates_hbm.1, bf16[16,256,256]{2,1,0:T(8,128)(2,1)} %band_hbm.1, ...), custom_call_target="tpu_custom_call" | custom-call | tf_op jit(solution)/shard_map/fused/pallas_call | solution.py:557
  72.6 0.9 %copy.14 = bf16[48,32,256]{2,1,0:T(8,128)(2,1)} copy(bf16[48,32,256]{2,1,0:T(8,128)(2,1)S(1)} %fused.1) | data formatting | bytes 1572864

commit v7 on v6

--- a/solution.py
+++ b/solution.py
@@ -151,8 +151,6 @@
     partners += [(gx, mod(gy + d, GY)) for d in range(2, GY - 1)]
     for device in partners:
         pl.semaphore_signal(barrier, inc=1, device_id=device, device_id_type=MESH)
-    for copy in w_copies[:1] + in_copies[9:] + in_copies[1:2] + w_copies[1:] + in_copies[2:9]:
-        copy.start()
 
     above = jnp.where(gx > 0, 1.0, 0.0)
     below = jnp.where(gx < GX - 1, 1.0, 0.0)
@@ -171,6 +169,8 @@
     pl.semaphore_wait(barrier, len(partners))
     halo, halo_all = border_copies(gx, gy, halo_out, halo_in, halo_s.at[0], halo_r.at[0])
     for copy in halo:
+        copy.start()
+    for copy in in_copies[1:2] + w_copies[:1] + in_copies[9:] + w_copies[1:] + in_copies[2:9]:
         copy.start()
     in_copies[1].wait()
     for b in (0, 2):

time: 73.7 us -> 73.8 us (level)
  no operation moved by 1% of the time
where the time goes in v7:
time: 73.8 us; the launch traced here: 73.5 us
  Pallas kernels  72.6 us (98%)
  local copies, waits for them, and re-layouts  0.88 us (1%)
    pallas_call x1, Pallas kernels, body(): pl.pallas_call(fused_body, name='fused', out_shape=pltpu.VMEM((ROWS, COLS...  72.6 us

profile of v7, /device:TPU:0, one launch (start us, length us, event | category | flops | bytes accessed | tf_op | source)
XLA Modules:
  0.0 73.5 jit_solution(11672697332339727223)
XLA Ops:
  0.0 72.6 %fused.1 = bf16[48,32,256]{2,1,0:T(8,128)(2,1)S(1)} custom-call(bf16[48,32,256]{2,1,0:T(8,128)(2,1)} %mid_hbm.1, bf16[48,32,256]{2,1,0:T(8,128)(2,1)} %grad_hbm.1, bf16[10,2304,256]{2,1,0:T(8,128)(2,1)} %bitcast.2, s32[3,2,4]{2,1,0:T(2,128)} %routes_hbm.1, f32[3,2,6]{2,1,0:T(2,128)} %gates_hbm.1, bf16[16,256,256]{2,1,0:T(8,128)(2,1)} %band_hbm.1, ...), custom_call_target="tpu_custom_call" | custom-call | tf_op jit(solution)/shard_map/fused/pallas_call | solution.py:557
  72.6 0.9 %copy.14 = bf16[48,32,256]{2,1,0:T(8,128)(2,1)} copy(bf16[48,32,256]{2,1,0:T(8,128)(2,1)S(1)} %fused.1) | data formatting | bytes 1572864
